TPU v7x, 32 devices: a whole 2x2x4 slice. The times are simulated.
32 devices in a mesh: videos: 2 (over y), tm: 8 (over z, x), tile: 2 (over core).
Axes of the slice: x: 2, y: 2, z: 4, core: 2. Of those that a mesh axis runs over, the one named last changes fastest.
Arguments:
- latents: bfloat16 [32, 8, 32, 384], P(('videos', 'tm'), None, 'tile'), parts along dimension 0, may hold values from -6 to 6, as said below
- frame_counts: int32 [16], P(('videos', 'tm')), parts along dimension 0, may hold values from 1 to 2, as said below
- owners: int32 [32], P('videos'), parts along dimension 0, may hold values from 0 to 1
- w_time: bfloat16 [3, 384, 768], replicated, may hold values from -0.1875 to 0.1875
- b_time: float32 [768], replicated, may hold values from -3 to 3
- w_up: bfloat16 [3, 3, 384, 192], replicated, may hold values from -0.109375 to 0.109375
- b_up: float32 [192], replicated, may hold values from -3 to 3
Outputs:
- decoded: bfloat16 [64, 16, 12288], P(('videos', 'tm'), None, 'tile'), parts along dimension 0
There are 2 independent parts, one for each index of `videos`. A program takes and returns all parts, laid end to end along the dimension named above; an argument that names none is the same for every part. Nothing has to cross between parts.
Inputs may be any that keep to these rules, and one draw needn't show every extreme that they name: `frame_counts`: every device has one or two valid frames; in every draw some device has two and some has one. `latents`: in every slot and row, stored columns 12 to 15 of tile 0 equal the first 4 stored columns of tile 1.
All inputs are finite; a program needn't handle non-finite values.
Results may differ from a plain program's by a relative error of at most 0.0047.
Values may be sent and summed in bfloat16 or wider, within the bound.
No kernel may reach another device: no remote copies, remote signals or barrier semaphores. Data moves between devices by JAX's collectives and lax.ppermute only.
A program may use at most 128 MiB of HBM per device.

v0:
```python
import jax
import jax.numpy as jnp
from jax import lax
from jax.sharding import PartitionSpec as P

OV = 4


def entering(x, axis, combine, identity):
    count, place = (lax.axis_size(axis), lax.axis_index(axis))
    everything = jax.tree.map(lambda part: lax.all_gather(part, axis), x)
    start = jax.tree.map(
        lambda part, zero: jnp.broadcast_to(jnp.asarray(zero, part.dtype), part.shape), x, identity
    )

    def step(k, before):
        reached = k < place
        new = combine(before, jax.tree.map(lambda part: part[k], everything))
        return jax.tree.map(lambda a, b: jnp.where(reached, a, b), new, before)

    return lax.fori_loop(0, count, step, start)


def partner(block, axis, apart):
    count = lax.axis_size(axis)
    route = []
    for low in range(count):
        high = low | 1 << apart
        if high != low and high < count:
            route += [(low, high), (high, low)]
    return lax.ppermute(block, axis, route)


def to_frames(tconv):
    count, rows, cols, both = tconv.shape
    half = both // 2
    return (
        tconv.reshape(count, rows, cols, 2, half)
        .transpose(0, 3, 1, 2, 4)
        .reshape(2 * count, rows, cols, half)
    )


def upconv(frames, w_up, b_up):
    count, rows, cols, chans = frames.shape
    big = jnp.repeat(jnp.repeat(frames, 2, axis=1), 2, axis=2)
    padded = jnp.pad(big, ((0, 0), (1, 1), (1, 1), (0, 0)))
    outc = w_up.shape[3]
    total = jnp.zeros((count * 4 * rows * cols, outc), jnp.float32)
    for row_tap in range(3):
        pieces = jnp.concatenate(
            [
                padded[:, row_tap : row_tap + 2 * rows, col_tap : col_tap + 2 * cols, :]
                for col_tap in range(3)
            ],
            -1,
        )
        total = total + jnp.dot(
            pieces.reshape(-1, 3 * chans),
            w_up[row_tap].reshape(3 * chans, outc),
            preferred_element_type=jnp.float32,
        )
    total = total + b_up
    return total.reshape(count, 2 * rows, 2 * cols, outc).astype(jnp.bfloat16)


def keep_latest(earlier, later):
    early_old, early_new, early_count = earlier
    late_old, late_new, late_count = later
    both_late = late_count[0] >= 1.5
    one_late = late_count[0] >= 0.5
    older = jnp.where(both_late, late_old, jnp.where(one_late, early_new, early_old))
    newer = jnp.where(one_late, late_new, early_new)
    merged = jnp.minimum(
        early_count.astype(jnp.float32) + late_count.astype(jnp.float32), 2.0
    ).astype(jnp.bfloat16)
    return (older, newer, merged)


def per_device(latents, frame_counts, owners, w_time, b_time, w_up, b_up):
    slot_total, rows, cols, chans = latents.shape
    count = frame_counts[0]
    blank = jnp.zeros_like(latents[0])
    latest = jnp.where(count >= 2, latents[1], latents[0])
    before = jnp.where(count >= 2, latents[0], blank)
    count_mark = jnp.minimum(count, 2).astype(jnp.bfloat16).reshape(1)
    older, newer, _unused = entering(
        (before, latest, count_mark),
        "tm",
        keep_latest,
        (blank, blank, jnp.zeros((1,), jnp.bfloat16)),
    )
    ext = jnp.concatenate([older[None], newer[None], latents], 0)
    stacked = jnp.concatenate(
        [ext[0:slot_total], ext[1 : slot_total + 1], ext[2 : slot_total + 2]], -1
    )
    tconv = (
        jnp.dot(
            stacked.reshape(-1, 3 * chans),
            w_time.reshape(3 * chans, 2 * chans),
            preferred_element_type=jnp.float32,
        )
        + b_time
    )
    tconv = tconv.reshape(slot_total, rows, cols, 2 * chans).astype(jnp.bfloat16)
    frames = to_frames(tconv)
    decoded = upconv(frames, w_up, b_up)
    outc = decoded.shape[3]
    wide = 2 * cols
    strip = 2 * OV
    mine = lax.axis_index("tile")
    own_strip = jnp.where(mine == 0, decoded[:, :, wide - strip :, :], decoded[:, :, :strip, :])
    other_strip = partner(own_strip, "tile", 0)
    left_strip = jnp.where(mine == 0, own_strip, other_strip).astype(jnp.float32)
    right_strip = jnp.where(mine == 0, other_strip, own_strip).astype(jnp.float32)
    weight = (strip - jnp.arange(strip, dtype=jnp.float32) - 0.5) / strip
    blend = left_strip * weight[:, None] + right_strip * (1.0 - weight[:, None])
    keep = (owners == mine)[None, :, None, None]
    placed = jnp.where(keep, blend, 0.0)
    full = decoded.astype(jnp.float32)
    as_left = full.at[:, :, wide - strip :, :].set(placed)
    as_right = full.at[:, :, :strip, :].set(placed)
    result = jnp.where(mine == 0, as_left, as_right)
    frame_slot = jnp.arange(2 * slot_total, dtype=jnp.int32) // 2
    result = jnp.where((frame_slot < count)[:, None, None, None], result, 0.0)
    return result.reshape(2 * slot_total, 2 * rows, wide * outc).astype(jnp.bfloat16)


def solution(mesh):
    placed = (
        P(("videos", "tm"), None, "tile", None),
        P(("videos", "tm")),
        P("videos"),
        P(),
        P(),
        P(),
        P(),
    )
    return jax.shard_map(
        per_device,
        mesh=mesh,
        in_specs=placed,
        out_specs=P(("videos", "tm"), None, "tile"),
        check_vma=False,
    )
```

profile of v0, /device:TPU:0, one launch (start us, length us, event | category | flops | bytes accessed | tf_op | source)
XLA Modules:
  0.0 137.9 jit_solution(17076122536966018167)
XLA Ops:
  0.8 1.2 dynamic-slice.15
  2.7 23.1 %all-reduce.1 = bf16[8]{0:T(256)(128)(2,1)S(1)} all-reduce(bf16[8]{0:T(256)(128)(2,1)S(1)} %dynamic-update-slice.6), channel_id=1, replica_groups=mesh['videos'=2,'tm'=8,'tile'=2] {'tm'}, use_global_device_ids=true, to_apply=%add.1 | all-reduce | flops 8 | bytes 32
  25.8 1.0 slice_select_fusion.1
  26.8 32.4 %all_gather.12 = bf16[8,8,16,384]{3,2,1,0:T(8,128)(2,1)S(1)} all-gather(bf16[1,8,16,384]{3,2,1,0:T(8,128)(2,1)S(1)} %get-tuple-element.212), channel_id=1, replica_groups=mesh['videos'=2,'tm'=8,'tile'=2] {'tm'}, dimensions={0}, use_global_device_ids=true | all-gather | bytes 884736 | tf_op jit(solution)/shard_map/all_gather | solution.py:11
  59.2 32.0 %all_gather.13 = bf16[8,8,16,384]{3,2,1,0:T(8,128)(2,1)S(1)} all-gather(bf16[1,8,16,384]{3,2,1,0:T(8,128)(2,1)S(1)} %get-tuple-element.211), channel_id=1, replica_groups=mesh['videos'=2,'tm'=8,'tile'=2] {'tm'}, dimensions={0}, use_global_device_ids=true | all-gather | bytes 884736 | tf_op jit(solution)/shard_map/all_gather | solution.py:11
  91.2 16.0 %while.18 = (s32[]{:T(128)}, bf16[8,16,384]{2,1,0:T(8,128)(2,1)S(1)}, bf16[8,16,384]{2,1,0:T(8,128)(2,1)S(1)}, s32[]{:T(128)}, bf16[8,1]{0,1:T(2,128)(2,1)S(1)},...) while((s32[]{:T(128)}, ...), condition=%wide.region_1.2_spmd.clone, body=%wide.region_0.1_spmd.clone.sunk | while | flops 344072 | bytes 589965 | solution.py:21
  92.5 0.7 select_select_fusion.2
  94.5 0.7 select_select_fusion.2
  96.5 0.7 select_select_fusion.2
  98.5 0.7 select_select_fusion.2
  106.5 0.7 select_select_fusion.2
  107.2 1.1 fusion.21
  109.2 1.1 broadcast_in_dim.53
  110.2 1.5 %reshape.136 = bf16[4,16,32,384]{3,2,1,0:T(8,128)(2,1)} reshape(bf16[4,16,16,2,384]{4,3,2,1,0:T(2,128)(2,1)S(1)} %broadcast_in_dim.53) | data formatting | bytes 3145728 | tf_op jit(solution)/shard_map/reshape | solution.py:46
  111.8 1.5 %concatenate.39 = bf16[2048,384]{1,0:T(8,128)(2,1)} reshape(bf16[4,16,16,2,384]{4,3,2,1,0:T(2,128)(2,1)S(1)} %broadcast_in_dim.53) | data formatting | bytes 3145728 | tf_op jit(solution)/shard_map/concatenate | solution.py:51
  113.3 8.3 %pad_slice_fusion.4 = (bf16[4,16,32,384]{3,2,1,0:T(8,128)(2,1)S(1)}, bf16[4,16,32,384]{3,2,1,0:T(8,128)(2,1)S(1)}, bf16[4,16,32,384]{3,2,1,0:T(8,128)(2,1)S(1)},...) fusion(bf16[4,16,32,384]{3,2,1,0:T(8,128)(2,1)} %reshape.136), kind=kLoop, calls=%fused_computation.17 | loop fusion | bytes 14155776 | tf_op jit(solution)/shard_map/slice | solution.py:53
  123.1 0.9 pad_maximum_fusion
  124.0 1.7 %fusion.29 = f32[2048,192]{0,1:T(8,128)S(1)} fusion(bf16[2048,1152]{1,0:T(8,128)(2,1)S(1)} %bitcast.59, bf16[1152,192]{0,1:T(8,128)(2,1)S(1)} %bitcast.69), kind=kOutput, calls=%fused_computation.52 | convolution fusion | flops 905969664 | bytes 6733824 | tf_op jit(solution)/shard_map/dot_general | solution.py:58
  125.7 1.7 %fusion.30 = f32[2048,192]{0,1:T(8,128)S(1)} fusion(bf16[2048,1152]{1,0:T(8,128)(2,1)S(1)} %bitcast.58, bf16[1152,192]{0,1:T(8,128)(2,1)S(1)} %bitcast.70), kind=kOutput, calls=%fused_computation.53 | convolution fusion | flops 905969664 | bytes 6733824 | tf_op jit(solution)/shard_map/dot_general | solution.py:58
  127.5 2.7 %fusion.16 = bf16[2048,192]{0,1:T(8,128)(2,1)} fusion(f32[2048,192]{0,1:T(8,128)S(1)} %fusion.30, f32[2048,192]{0,1:T(8,128)S(1)} %fusion.29, bf16[1152,192]{0,1:T(8,128)(2,1)S(1)} %bitcast.75, bf16[2048,384]{1,0:T(8,128)(2,1)S(1)} %bitcast.72, bf16[2048,384]{1,0:T(8,128)(2,1)S(1)} %copy-done.1, bf16[2048,384]{1,0:T(8,128)(2,1)S(1)} %bitcast.71, ...), kind=kOutput, calls=%fused_computation.24 | convolution fusion | flops 921698304 | bytes 9093888 | tf_op jit(solution)/shard_map/dot_general | solution.py:58
  130.2 1.4 %copy.16 = bf16[2048,192]{1,0:T(8,128)(2,1)S(1)} copy(bf16[2048,192]{0,1:T(8,128)(2,1)} %fusion.16) | data formatting | bytes 1572864 | tf_op jit(solution)/shard_map/convert_element_type | solution.py:64
  132.3 1.0 collective-permute-done
  133.6 1.5 %select_convert_fusion = bf16[4,16,32,192]{3,2,1,0:T(8,128)(2,1)} fusion(bf16[4,16,32,192]{3,2,1,0:T(8,128)(2,1)S(1)} %fusion.23, bf16[4,16,32,192]{3,2,1,0:T(8,128)(2,1)S(1)} %fusion.22, pred[4]{0:T(512)(128)(4,1)S(1)} %fusion.24, pred[]{:T(512)S(6)} %eq.12), kind=kLoop, calls=%fused_computation.25 | loop fusion | flops 786432 | bytes 2359301 | tf_op jit(solution)/shard_map/convert_element_type | solution.py:126
  135.1 2.9 %convert_element_type.41 = bf16[4,16,6144]{2,1,0:T(8,128)(2,1)} reshape(bf16[4,16,32,192]{3,2,1,0:T(8,128)(2,1)} %select_convert_fusion) | data formatting | bytes 1572864 | tf_op jit(solution)/shard_map/convert_element_type | solution.py:126
  (46 shorter events, 11.2 us)
Async XLA Ops:
  0.0 108.3 %copy-start = (bf16[3,384,768]{2,1,0:T(8,128)(2,1)S(1)}, bf16[3,384,768]{2,1,0:T(8,128)(2,1)}, u32[]{:S(2)}) copy-start(bf16[3,384,768]{2,1,0:T(8,128)(2,1)} %param.16) | copy-start | bytes 5308420
  91.2 17.1 %copy-start.3 = (f32[768]{0:T(1024)S(1)}, f32[768]{0:T(1024)}, u32[]{:S(2)}) copy-start(f32[768]{0:T(1024)} %param.17) | copy-start | bytes 9220
  113.3 8.3 %copy-start.2 = (bf16[3,3,384,192]{2,3,1,0:T(8,128)(2,1)S(1)}, bf16[3,3,384,192]{2,3,1,0:T(8,128)(2,1)}, u32[]{:S(2)}) copy-start(bf16[3,3,384,192]{2,3,1,0:T(8,128)(2,1)} %param.18) | copy-start | bytes 3981316
  125.7 1.8 %copy-start.1 = (bf16[2048,384]{1,0:T(8,128)(2,1)S(1)}, bf16[2048,384]{1,0:T(8,128)(2,1)}, u32[]{:S(2)}) copy-start(bf16[2048,384]{1,0:T(8,128)(2,1)} %concatenate.39) | copy-start | bytes 4718596
  125.7 1.8 %copy-start.4 = (f32[192]{0:T(256)S(1)}, f32[192]{0:T(256)}, u32[]{:S(2)}) copy-start(f32[192]{0:T(256)} %param.19) | copy-start | bytes 2308
  131.6 0.7 copy-start.5
  131.7 1.6 %collective-permute-start = (bf16[4,16,8,192]{3,2,1,0:T(8,128)(2,1)S(1)}, bf16[4,16,8,192]{3,2,1,0:T(8,128)(2,1)S(1)}, u32[]{:S(2)}, u32[]{:S(2)}) collective-permute-start(bf16[4,16,8,192]{3,2,1,0:T(8,128)(2,1)S(1)} %slice_select_fusion), channel_id=1, source_target_pairs={{0,1},{1,0},{2,3},{3,2},{4,5},{5,4},{6,7},{7,6},{8,9},{9,8},{10,11... | collective-permute-start | bytes 589832 | tf_op jit(solution)/shard_map/ppermute | solution.py:31
where the time goes:
time: 138 us
  blocking collectives  87.5 us (63%)
  local copies, waits for them, and re-layouts  20.7 us (15%)
  other arithmetic  15.6 us (11%)
  matrix products  6.78 us (5%)
  loops' own time  5.24 us (4%)
    all_gather x2, blocking collectives, entering(): everything = jax.tree.map(lambda part: lax.all_gather(part, axis), x)  64.4 us
    unnamed x1, blocking collectives  23.1 us
    slice x1, local copies, waits for them, and re-layouts, upconv(): padded[:, row_tap:row_tap + 2 * rows, col_tap:col_tap + 2 * cols, :]  8.31 us
    dot_general x3, matrix products, upconv(): jnp.dot(pieces.reshape(-1, 3 * chans), w_up[row_tap].reshape(3 * chans, o...  6.11 us
    select_n x8, other arithmetic, step(): return jax.tree.map(lambda a, b: jnp.where(reached, a, b), new, before)  5.58 us
    another operation x1, loops' own time, entering(): return lax.fori_loop(0, count, step, start)  5.24 us
    ge x8, other arithmetic, keep_latest(): one_late = late_count[0] >= 0.5  5.19 us
    convert_element_type x1, local copies, waits for them, and re-layouts, per_device(): result.reshape(2 * slot_total, 2 * rows, wide * outc).astype(jnp.bfloat16)  2.86 us
  transfers between devices with their start and end apart: 1, of which 1 were waited for; matrix products, arithmetic and copies ran while one was open for 0% of the time, Pallas kernels for 0%

commit v1 on v0

v1 whole, which is shorter than its diff:
```python
import functools

import jax
import jax.numpy as jnp
from jax import lax
from jax.experimental import pallas as pl
from jax.experimental.pallas import tpu as pltpu
from jax.sharding import PartitionSpec as P

OV = 4
F32 = jnp.float32
BF16 = jnp.bfloat16


def dot(a, b):
    return jnp.dot(a, b, preferred_element_type=F32)


def prepare_weights(w_up, wc, wl, wr):
    chans, outc = w_up.shape[2], w_up.shape[3]
    blank = jnp.zeros((chans, 64), F32)
    for pr, block, rows in ((0, 0, (0,)), (0, 1, (1, 2)), (1, 0, (0, 1)), (1, 1, (2,))):
        taps = []
        for col in range(3):
            tap = w_up[rows[0], col].astype(F32)
            for row in rows[1:]:
                tap = tap + w_up[row, col].astype(F32)
            taps.append(tap)
        span = pl.ds(block * chans, chans)
        wc[pr, span, :] = jnp.concatenate([taps[1] + taps[2], taps[0] + taps[1]], -1).astype(BF16)
        wl[pr, span, :] = jnp.concatenate([taps[0], blank], -1).astype(BF16)
        wr[pr, span, :] = jnp.concatenate([blank, taps[2]], -1).astype(BF16)


def placement(rows, cols):
    height, depth = 3 * cols * 2 * rows, 2 * rows * cols
    i = lax.broadcasted_iota(jnp.int32, (height, depth), 0)
    k = lax.broadcasted_iota(jnp.int32, (height, depth), 1)
    group = cols * 2 * rows
    shift = i // group
    col = (i % group) // (2 * rows)
    half = (i % (2 * rows)) // rows
    row = i % rows + shift - 1
    hit = (k == half * rows * cols + row * cols + col) & (row >= 0) & (row < rows)
    return jnp.where(hit, 1.0, 0.0).astype(BF16)


def picker(rows, cols, col):
    i = lax.broadcasted_iota(jnp.int32, (2 * rows, rows * cols), 0)
    k = lax.broadcasted_iota(jnp.int32, (2 * rows, rows * cols), 1)
    return jnp.where((i < rows) & (k == i * cols + col), 1.0, 0.0).astype(BF16)


def row_shifts(t):
    row = lax.broadcasted_iota(jnp.int32, t.shape, 0)
    up = jnp.where(row == 0, 0.0, pltpu.roll(t, 1, 0))
    down = jnp.where(row == t.shape[0] - 1, 0.0, pltpu.roll(t, t.shape[0] - 1, 0))
    return up, t, down


def fill_x(t, mine, place, x, rows, cols):
    chans = t.shape[1] // 2
    pixels = rows * cols
    body = t[:pixels].astype(BF16)
    both = jnp.concatenate([body[:, :chans], body[:, chans:]], 0)
    spread = dot(place, both).astype(BF16)
    height = 2 * pixels
    edge = t[pixels : pixels + rows].astype(BF16).astype(F32)
    for v, shifted in enumerate(row_shifts(edge)):
        lanes = pl.ds(v * chans, chans)
        x[pl.ds(2 * rows, height), lanes] = spread[v * height : (v + 1) * height]
        column = jnp.concatenate([shifted[:, :chans], shifted[:, chans:]], 0)
        x[pl.ds(0, 2 * rows), lanes] = jnp.where(mine == 1, column, 0.0).astype(BF16)
        x[pl.ds(2 * rows + height, 2 * rows), lanes] = jnp.where(mine == 0, column, 0.0).astype(BF16)


def convolve(x, wc, wl, wr, bias, owners, mine, valid, wide, out, first, rows, cols):
    chans2 = wc.shape[1]
    chans = chans2 // 2
    height = 2 * rows * cols
    lanes = wc.shape[2]
    part = wl.shape[2]
    col_of = lax.broadcasted_iota(jnp.int32, (height, 1), 0) // (2 * rows)
    strip_from = jnp.where(mine == 0, cols - OV, 0)
    soft = 1.0 - 0.5 / (2 * OV)
    scale_l = jnp.where(col_of == strip_from, soft, 1.0)
    scale_r = jnp.where(col_of == strip_from + OV - 1, soft, 1.0)
    for pr in range(2):
        span = pl.ds(pr * chans, chans2)
        mid = dot(x[pl.ds(2 * rows, height), span], wc[pr])
        left = dot(x[pl.ds(0, height), span], wl[pr]) * scale_l
        right = dot(x[pl.ds(4 * rows, height), span], wr[pr]) * scale_r
        low = mid[:, : lanes - part] + left[:, : lanes - part]
        centre = mid[:, lanes - part : part] + left[:, lanes - part :] + right[:, : 2 * part - lanes]
        high = mid[:, part:] + right[:, 2 * part - lanes :]
        y = jnp.concatenate([low, centre, high], -1) + bias
        for col in range(cols):
            for h in range(2):
                top = col * 2 * rows + h * rows
                for j in range(lanes // 128):
                    wide[h, col * lanes // 128 + j, pl.ds(pr, rows, stride=2), :] = y[
                        top : top + rows, j * 128 : (j + 1) * 128
                    ]
    out_row = lax.broadcasted_iota(jnp.int32, (2 * rows, 128), 0)
    keep = jnp.zeros((2 * rows, 128), jnp.int32)
    for r in range(2 * rows):
        keep = jnp.where(out_row == r, owners[r], keep)
    keep = jnp.where(keep == mine, 1.0, 0.0)
    shown = jnp.where(valid, 1.0, 0.0)
    for col in range(cols):
        in_strip = (col >= strip_from) & (col < strip_from + OV)
        mask = jnp.where(in_strip, keep, 1.0) > 0.5
        for h in range(2):
            for lane in range(col * lanes, (col + 1) * lanes, 128):
                block = wide[h, lane // 128]
                block = jnp.where(mask & (shown > 0.5), block, 0.0)
                out[first + h, :, pl.ds(lane, 128)] = block.astype(BF16)


def kernel(
    facts, owners, own, own_far, near, near_far, far, far_far, w_time, b_time, w_up, b_up,
    out, lhs, x, wc, wl, wr, wide,
):
    slots, rows, cols, chans = own.shape
    pixels = rows * cols
    mine, count, count_near, place_tm = facts[0], facts[1], facts[2], facts[3]
    prepare_weights(w_up, wc, wl, wr)
    pick = picker(rows, cols, jnp.where(mine == 0, OV, cols - OV - 1))

    def fill(k, main, other, on):
        main = jnp.where(on, main, jnp.zeros_like(main))
        other = jnp.where(on, other, jnp.zeros_like(other))
        lhs[k, pl.ds(0, pixels), :] = main
        lhs[k, pl.ds(pixels, 2 * rows), :] = dot(pick, other).astype(BF16)

    flat = lambda v: v.reshape(pixels, chans)
    near_two = count_near == 2
    older = jnp.where(near_two, flat(near[0]), flat(far[0]))
    older_far = jnp.where(near_two, flat(near_far[0]), flat(far_far[0]))
    newer = jnp.where(near_two, flat(near[1]), flat(near[0]))
    newer_far = jnp.where(near_two, flat(near_far[1]), flat(near_far[0]))
    fill(0, older, older_far, (place_tm >= 2) | ((place_tm == 1) & near_two))
    fill(1, newer, newer_far, place_tm >= 1)
    fill(2, flat(own[0]), flat(own_far[0]), place_tm >= 0)
    fill(3, flat(own[1]), flat(own_far[1]), place_tm >= 0)
    place = placement(rows, cols)
    bias = jnp.concatenate([b_up[...], b_up[...]], -1)
    for slot in range(2):
        t = b_time[...] + dot(lhs[slot], w_time[0])
        t = t + dot(lhs[slot + 1], w_time[1])
        t = t + dot(lhs[slot + 2], w_time[2])
        fill_x(t, mine, place, x, rows, cols)
        convolve(x, wc, wl, wr, bias, owners, mine, slot < count, wide, out, 2 * slot, rows, cols)


def per_device(latents, frame_counts, owners, w_time, b_time, w_up, b_up):
    slots, rows, cols, chans = latents.shape
    outc = w_up.shape[3]
    ring = lax.axis_size("tm")
    place_tm = lax.axis_index("tm")
    mine = lax.axis_index("tile")
    count = frame_counts[0]
    other = [(0, 1), (1, 0)]
    step = lambda k: [(i, (i + k) % ring) for i in range(ring)]
    near = lax.ppermute(latents, "tm", step(1))
    latest = lax.dynamic_slice_in_dim(latents, count - 1, 1, 0)
    far = lax.ppermute(latest, "tm", step(2))
    count_near = lax.ppermute(frame_counts, "tm", step(1))
    own_far = lax.ppermute(latents, "tile", other)
    near_far = lax.ppermute(near, "tile", other)
    far_far = lax.ppermute(far, "tile", other)
    facts = jnp.stack([mine, count, count_near[0], place_tm]).astype(jnp.int32)
    smem = pl.BlockSpec(memory_space=pltpu.SMEM)
    vmem = pl.BlockSpec(memory_space=pltpu.VMEM)
    wide_lanes = 2 * cols * outc
    return pl.pallas_call(
        kernel,
        out_shape=jax.ShapeDtypeStruct((2 * slots, 2 * rows, wide_lanes), BF16),
        in_specs=[smem, smem] + [vmem] * 10,
        out_specs=vmem,
        scratch_shapes=[
            pltpu.VMEM((4, rows * cols + 2 * rows, chans), BF16),
            pltpu.VMEM(((cols + 2) * 2 * rows, 3 * chans), BF16),
            pltpu.VMEM((2, 2 * chans, 2 * outc), BF16),
            pltpu.VMEM((2, 2 * chans, 256), BF16),
            pltpu.VMEM((2, 2 * chans, 256), BF16),
            pltpu.VMEM((2, wide_lanes // 128, 2 * rows, 128), F32),
        ],
        compiler_params=pltpu.CompilerParams(vmem_limit_bytes=40 << 20),
        cost_estimate=pl.CostEstimate(flops=2 * 10**9, bytes_accessed=4 << 20, transcendentals=0),
    )(
        facts, owners, latents, own_far, near, near_far, far, far_far,
        w_time, b_time.reshape(1, -1), w_up, b_up.reshape(1, -1),
    )


def solution(mesh):
    placed = (
        P(("videos", "tm"), None, "tile", None),
        P(("videos", "tm")),
        P("videos"),
        P(),
        P(),
        P(),
        P(),
    )
    return jax.shard_map(
        per_device,
        mesh=mesh,
        in_specs=placed,
        out_specs=P(("videos", "tm"), None, "tile"),
        check_vma=False,
    )
```

time: 138 us -> 26.7 us (0.19)
  blocking collectives: 87.5 us -> 0 us
  local copies, waits for them, and re-layouts: 20.7 us -> 5.6 us
  other arithmetic: 15.6 us -> 0.7 us
  waiting for transfers between devices: 1 us -> 8.32 us
  matrix products: 6.78 us -> 0 us
  Pallas kernels: 0 us -> 5.93 us
  loops' own time: 5.24 us -> 0 us
  starting transfers between devices: 0.07 us -> 5.2 us
    all_gather x2 -> x0, blocking collectives: 64.4 us -> none  [entering(): everything = jax.tree.map(lambda part: lax.all_gather(part, axis), x)]
    unnamed x1 -> x0, blocking collectives: 23.1 us -> none
    slice x5 -> x0, local copies, waits for them, and re-layouts: 9.59 us -> none  [the longest x1 8.31 us: upconv(): padded[:, row_tap:row_tap + 2 * rows, col_tap:col_tap + 2 * cols, :]]
    ppermute x1 -> x6, waiting for transfers between devices: 1 us -> 8.32 us  [the longest x1 5.79 us: per_device(): near = lax.ppermute(latents, 'tm', step(1))]
    dot_general x4 -> x0, matrix products: 6.78 us -> none  [the longest x3 6.11 us: upconv(): jnp.dot(pieces.reshape(-1, 3 * chans), w_up[row_tap].reshape(3 * chans, o...]
    select_n x10 -> x0, other arithmetic: 6.58 us -> none  [the longest x8 5.58 us: step(): return jax.tree.map(lambda a, b: jnp.where(reached, a, b), new, before)]
    pallas_call x0 -> x1, Pallas kernels: none -> 5.93 us  [per_device(): pl.pallas_call(kernel, out_shape=jax.ShapeDtypeStruct((2 * slots, 2 * row...]
    another operation x1 -> x0, loops' own time: 5.24 us -> none  [entering(): return lax.fori_loop(0, count, step, start)]
  transfers between devices with their start and end apart: 1 -> 6, of which waited for: 1 -> 2; matrix products, arithmetic and copies ran while one was open for 0% -> 18% of each run, Pallas kernels for 0% -> 0%
where the time goes in v1:
time: 26.7 us; the launch traced here: 26.5 us
  waiting for transfers between devices  8.32 us (31%)
  Pallas kernels  5.93 us (22%)
  local copies, waits for them, and re-layouts  5.6 us (21%)
  starting transfers between devices  5.2 us (19%)
  between operations  0.72 us (3%)
  other arithmetic  0.7 us (3%)
    pallas_call x1, Pallas kernels, per_device(): pl.pallas_call(kernel, out_shape=jax.ShapeDtypeStruct((2 * slots, 2 * row...  5.93 us
    ppermute x1, waiting for transfers between devices, per_device(): near = lax.ppermute(latents, 'tm', step(1))  5.79 us
    unnamed x9, local copies, waits for them, and re-layouts  4 us
    ppermute x1, starting transfers between devices, per_device(): near = lax.ppermute(latents, 'tm', step(1))  2.99 us
    ppermute x1, waiting for transfers between devices, per_device(): count_near = lax.ppermute(frame_counts, 'tm', step(1))  2.52 us
    ppermute x1, starting transfers between devices, per_device(): far = lax.ppermute(latest, 'tm', step(2))  1.63 us
    dynamic_slice x1, local copies, waits for them, and re-layouts, per_device(): latest = lax.dynamic_slice_in_dim(latents, count - 1, 1, 0)  0.91 us
    another operation x1, other arithmetic, per_device(): facts = jnp.stack([mine, count, count_near[0], place_tm]).astype(jnp.int32)  0.7 us
  transfers between devices with their start and end apart: 6, of which 2 were waited for; matrix products, arithmetic and copies ran while one was open for 18% of the time, Pallas kernels for 0%

profile of v1, /device:TPU:0, one launch (start us, length us, event | category | flops | bytes accessed | tf_op | source)
XLA Modules:
  0.0 26.5 jit_solution(8615811131848435704)
XLA Ops:
  0.0 0.0 copy-start
  0.0 0.0 copy-start.2
  0.0 3.0 %collective-permute-start.2 = (bf16[2,8,16,384]{3,2,1,0:T(8,128)(2,1)}, bf16[2,8,16,384]{3,2,1,0:T(8,128)(2,1)S(1)}, u32[]{:S(2)}, u32[]{:S(2)}) collective-permute-start(bf16[2,8,16,384]{3,2,1,0:T(8,128)(2,1)} %own.1), channel_id=1, source_target_pairs={{0,2},{2,4},{4,6},{6,8},{8,10},{10,12},{12,14},{14,0},{1,3},{3,5},... | collective-permute-start | bytes 589832 | tf_op jit(solution)/shard_map/ppermute | solution.py:165
  3.7 0.9 %constant_dynamic-slice_fusion = bf16[1,8,16,384]{3,2,1,0:T(8,128)(2,1)S(1)} fusion(bf16[2,8,16,384]{3,2,1,0:T(8,128)(2,1)} %own.1, s32[]{:T(128)S(6)} %select_n.3), kind=kLoop, calls=%fused_computation.1 | loop fusion | bytes 196612 | tf_op jit(solution)/shard_map/dynamic_slice | solution.py:166
  4.6 1.6 %collective-permute-start.4 = (bf16[1,8,16,384]{3,2,1,0:T(8,128)(2,1)S(1)}, bf16[1,8,16,384]{3,2,1,0:T(8,128)(2,1)S(1)}, u32[]{:S(2)}, u32[]{:S(2)}) collective-permute-start(bf16[1,8,16,384]{3,2,1,0:T(8,128)(2,1)S(1)} %constant_dynamic-slice_fusion), channel_id=1, source_target_pairs={{0,4},{2,6},{4,8},{6,10},{8,12},{10,14},{12,0},{14,2},{1,5},{3,7},... | collective-permute-start | bytes 294920 | tf_op jit(solution)/shard_map/ppermute | solution.py:167
  6.2 0.0 collective-permute-start.1
  6.2 5.8 %collective-permute-done.2.near = bf16[2,8,16,384]{3,2,1,0:T(8,128)(2,1)S(1)} collective-permute-done((bf16[2,8,16,384]{3,2,1,0:T(8,128)(2,1)}, bf16[2,8,16,384]{3,2,1,0:T(8,128)(2,1)S(1)}, u32[]{:S(2)}, u32[]{:S(2)}) %collective-permute-start.2) | collective-permute-done | bytes 196640 | tf_op jit(solution)/shard_map/ppermute | solution.py:165
  12.0 0.0 collective-permute-start.3
  12.0 0.0 collective-permute-start
  12.0 0.7 %reshape.10.b_time = f32[1,768]{1,0:T(1,128)S(1)} reshape(f32[768]{0:T(1024)} %param.11) | data formatting | bytes 6144 | tf_op jit(solution)/shard_map/reshape | solution.py:193
  12.7 2.5 %copy.8.w_up = bf16[3,3,384,192]{3,2,1,0:T(8,128)(2,1)S(1)} copy(bf16[3,3,384,192]{2,3,1,0:T(8,128)(2,1)} %param.12) | data formatting | bytes 2654208 | tf_op args[5]
  15.2 0.0 collective-permute-done.4.far
  15.2 0.6 %collective-permute-start.5 = (bf16[1,8,16,384]{3,2,1,0:T(8,128)(2,1)S(1)}, bf16[1,8,16,384]{3,2,1,0:T(8,128)(2,1)S(1)}, u32[]{:S(2)}, u32[]{:S(2)}) collective-permute-start(bf16[1,8,16,384]{3,2,1,0:T(8,128)(2,1)S(1)} %collective-permute-done.4.far), channel_id=1, source_target_pairs={{0,1},{1,0},{2,3},{3,2},{4,5},{5,4},{6,7},{7,6},{8,9},{9,8},{10,11... | collective-permute-start | bytes 294920 | tf_op jit(solution)/shard_map/ppermute | solution.py:171
  15.8 2.5 %collective-permute-done = s32[1]{0:T(128)} collective-permute-done((s32[1]{0:T(128)}, s32[1]{0:T(128)}, u32[]{:S(2)}, u32[]{:S(2)}) %collective-permute-start) | collective-permute-done | bytes 36 | tf_op jit(solution)/shard_map/ppermute | solution.py:168
  18.3 0.7 %pad_add_fusion.facts = s32[4]{0:T(128)S(1)} fusion(s32[1]{0:T(128)} %bitcast.1, s32[1]{0:T(128)} %collective-permute-done, s32[1]{0:T(128)S(6)} %copy.9, s32[1]{0:T(128)} %bitcast), kind=kLoop, calls=%fused_computation | loop fusion | flops 12 | bytes 32 | tf_op jit(solution)/shard_map/stack | solution.py:172
  19.0 0.0 collective-permute-done.5.far_far
  19.0 0.0 collective-permute-done.1.own_far
  19.0 0.0 collective-permute-done.3.near_far
  19.0 0.0 copy-done
  19.0 0.0 copy-done.2
  19.1 0.0 copy-done.3
  19.1 0.0 copy-start.1
  19.1 1.5 %copy-done.1 = bf16[3,384,768]{2,1,0:T(8,128)(2,1)S(1)} copy-done((bf16[3,384,768]{2,1,0:T(8,128)(2,1)S(1)}, bf16[3,384,768]{2,1,0:T(8,128)(2,1)}, u32[]{:S(2)}) %copy-start.1) | copy-done | bytes 1769496
  20.5 5.9 %shard_map.73 = bf16[4,16,6144]{2,1,0:T(8,128)(2,1)} custom-call(s32[4]{0:T(128)S(1)} %pad_add_fusion.facts, s32[16]{0:T(128)S(1)} %copy-done.3, bf16[2,8,16,384]{3,2,1,0:T(8,128)(2,1)S(1)} %copy-done, bf16[2,8,16,384]{3,2,1,0:T(8,128)(2,1)S(1)} %collective-permute-done.1.own_far, bf16[2,8,16,384]{3,2,1,0:T(8,128)(2,1)S(1)} %collective-permute-done.2.near, ...), custom_call_target="tpu_custom_call" | custom-call | flops 2000000000 | bytes 4194304 | tf_op jit(solution)/shard_map/pallas_call | solution.py:176
  (1 shorter events, 0.0 us)
Async XLA Ops:
  0.0 19.0 %copy-start = (bf16[2,8,16,384]{3,2,1,0:T(8,128)(2,1)S(1)}, bf16[2,8,16,384]{3,2,1,0:T(8,128)(2,1)}, u32[]{:S(2)}) copy-start(bf16[2,8,16,384]{3,2,1,0:T(8,128)(2,1)} %own.1) | copy-start | bytes 589828
  0.0 19.0 %copy-start.2 = (f32[192]{0:T(256)S(1)}, f32[192]{0:T(256)}, u32[]{:S(2)}) copy-start(f32[192]{0:T(256)} %param.13) | copy-start | bytes 2308
  0.0 19.0 %copy-start.3 = (s32[16]{0:T(128)S(1)}, s32[16]{0:T(128)}, u32[]{:S(2)}) copy-start(s32[16]{0:T(128)} %owners.1) | copy-start | bytes 196
  0.0 12.0 %collective-permute-start.2 = (bf16[2,8,16,384]{3,2,1,0:T(8,128)(2,1)}, bf16[2,8,16,384]{3,2,1,0:T(8,128)(2,1)S(1)}, u32[]{:S(2)}, u32[]{:S(2)}) collective-permute-start(bf16[2,8,16,384]{3,2,1,0:T(8,128)(2,1)} %own.1), channel_id=1, source_target_pairs={{0,2},{2,4},{4,6},{6,8},{8,10},{10,12},{12,14},{14,0},{1,3},{3,5},... | collective-permute-start | bytes 589832 | tf_op jit(solution)/shard_map/ppermute | solution.py:165
  4.6 10.6 %collective-permute-start.4 = (bf16[1,8,16,384]{3,2,1,0:T(8,128)(2,1)S(1)}, bf16[1,8,16,384]{3,2,1,0:T(8,128)(2,1)S(1)}, u32[]{:S(2)}, u32[]{:S(2)}) collective-permute-start(bf16[1,8,16,384]{3,2,1,0:T(8,128)(2,1)S(1)} %constant_dynamic-slice_fusion), channel_id=1, source_target_pairs={{0,4},{2,6},{4,8},{6,10},{8,12},{10,14},{12,0},{14,2},{1,5},{3,7},... | collective-permute-start | bytes 294920 | tf_op jit(solution)/shard_map/ppermute | solution.py:167
  6.2 12.8 %collective-permute-start.1 = (bf16[2,8,16,384]{3,2,1,0:T(8,128)(2,1)}, bf16[2,8,16,384]{3,2,1,0:T(8,128)(2,1)S(1)}, u32[]{:S(2)}, u32[]{:S(2)}) collective-permute-start(bf16[2,8,16,384]{3,2,1,0:T(8,128)(2,1)} %own.1), channel_id=1, source_target_pairs={{0,1},{1,0},{2,3},{3,2},{4,5},{5,4},{6,7},{7,6},{8,9},{9,8},{10,11... | collective-permute-start | bytes 589832 | tf_op jit(solution)/shard_map/ppermute | solution.py:169
  12.0 7.0 %collective-permute-start.3 = (bf16[2,8,16,384]{3,2,1,0:T(8,128)(2,1)S(1)}, bf16[2,8,16,384]{3,2,1,0:T(8,128)(2,1)S(1)}, u32[]{:S(2)}, u32[]{:S(2)}) collective-permute-start(bf16[2,8,16,384]{3,2,1,0:T(8,128)(2,1)S(1)} %collective-permute-done.2.near), channel_id=1, source_target_pairs={{0,1},{1,0},{2,3},{3,2},{4,5},{5,4},{6,7},{7,6},{8,9},{9,8},{10,11... | collective-permute-start | bytes 589832 | tf_op jit(solution)/shard_map/ppermute | solution.py:170
  12.0 6.3 %collective-permute-start = (s32[1]{0:T(128)}, s32[1]{0:T(128)}, u32[]{:S(2)}, u32[]{:S(2)}) collective-permute-start(s32[1]{0:T(128)} %param.8), channel_id=1, source_target_pairs={{0,2},{2,4},{4,6},{6,8},{8,10},{10,12},{12,14},{14,0},{1,3},{3,5},... | collective-permute-start | bytes 20 | tf_op jit(solution)/shard_map/ppermute | solution.py:168
  15.2 3.8 %collective-permute-start.5 = (bf16[1,8,16,384]{3,2,1,0:T(8,128)(2,1)S(1)}, bf16[1,8,16,384]{3,2,1,0:T(8,128)(2,1)S(1)}, u32[]{:S(2)}, u32[]{:S(2)}) collective-permute-start(bf16[1,8,16,384]{3,2,1,0:T(8,128)(2,1)S(1)} %collective-permute-done.4.far), channel_id=1, source_target_pairs={{0,1},{1,0},{2,3},{3,2},{4,5},{5,4},{6,7},{7,6},{8,9},{9,8},{10,11... | collective-permute-start | bytes 294920 | tf_op jit(solution)/shard_map/ppermute | solution.py:171
  19.1 1.5 %copy-start.1 = (bf16[3,384,768]{2,1,0:T(8,128)(2,1)S(1)}, bf16[3,384,768]{2,1,0:T(8,128)(2,1)}, u32[]{:S(2)}) copy-start(bf16[3,384,768]{2,1,0:T(8,128)(2,1)} %w_time.1) | copy-start | bytes 5308420

commit v2 on v1

v2 whole, which is shorter than its diff:
```python
import jax
import jax.numpy as jnp
from jax import lax
from jax.experimental import pallas as pl
from jax.experimental.pallas import tpu as pltpu
from jax.sharding import PartitionSpec as P

OV = 4
F32 = jnp.float32
BF16 = jnp.bfloat16
VMEM = pl.BlockSpec(memory_space=pltpu.VMEM)
SMEM = pl.BlockSpec(memory_space=pltpu.SMEM)
ANY = pl.BlockSpec(memory_space=pl.ANY)
PARAMS = pltpu.CompilerParams(vmem_limit_bytes=24 << 20)


def dot(a, b):
    return jnp.dot(a, b, preferred_element_type=F32)


def dot_t(a, b):
    return lax.dot_general(a, b, (((1,), (1,)), ((), ())), preferred_element_type=F32)


def cost(flops, moved):
    return pl.CostEstimate(flops=flops, bytes_accessed=moved, transcendentals=0)


def prepare_weights(w_up, wc, wl, wr):
    outc, chans = w_up.shape[2], w_up.shape[3]
    pad = wl.shape[1] - outc
    for pr, block, rows in ((0, 0, (0,)), (0, 1, (1, 2)), (1, 0, (0, 1)), (1, 1, (2,))):
        taps = []
        for col in range(3):
            tap = w_up[rows[0], col].astype(F32)
            for row in rows[1:]:
                tap = tap + w_up[row, col].astype(F32)
            taps.append(tap)
        span = pl.ds(block * chans, chans)
        wc[pr, pl.ds(0, outc), span] = (taps[1] + taps[2]).astype(BF16)
        wc[pr, pl.ds(outc, outc), span] = (taps[0] + taps[1]).astype(BF16)
        wl[pr, pl.ds(0, outc), span] = taps[0].astype(BF16)
        wl[pr, pl.ds(outc, pad), span] = jnp.zeros((pad, chans), BF16)
        wr[pr, pl.ds(0, pad), span] = jnp.zeros((pad, chans), BF16)
        wr[pr, pl.ds(pad, outc), span] = taps[2].astype(BF16)


def placement(rows, cols):
    height, depth = 3 * cols * 2 * rows, 2 * rows * cols
    i = lax.broadcasted_iota(jnp.int32, (height, depth), 0)
    k = lax.broadcasted_iota(jnp.int32, (height, depth), 1)
    group = cols * 2 * rows
    shift = i // group
    col = (i % group) // (2 * rows)
    half = (i % (2 * rows)) // rows
    row = i % rows + shift - 1
    hit = (k == half * rows * cols + row * cols + col) & (row >= 0) & (row < rows)
    return jnp.where(hit, 1.0, 0.0).astype(BF16)


def picker(rows, cols, col):
    i = lax.broadcasted_iota(jnp.int32, (2 * rows, rows * cols), 0)
    k = lax.broadcasted_iota(jnp.int32, (2 * rows, rows * cols), 1)
    return jnp.where((i < rows) & (k == i * cols + col), 1.0, 0.0).astype(BF16)


def row_shifts(t):
    row = lax.broadcasted_iota(jnp.int32, t.shape, 0)
    up = jnp.where(row == 0, 0.0, pltpu.roll(t, 1, 0))
    down = jnp.where(row == t.shape[0] - 1, 0.0, pltpu.roll(t, t.shape[0] - 1, 0))
    return up, t, down


def fill_x(t, mine, place, x, rows, cols):
    chans = t.shape[1] // 2
    pixels = rows * cols
    body = t[:pixels].astype(BF16)
    both = jnp.concatenate([body[:, :chans], body[:, chans:]], 0)
    height = 2 * pixels
    edge = t[pixels : pixels + rows].astype(BF16).astype(F32)
    for v, shifted in enumerate(row_shifts(edge)):
        lanes = pl.ds(v * chans, chans)
        x[pl.ds(2 * rows, height), lanes] = dot(place[pl.ds(v * height, height), :], both).astype(BF16)
        column = jnp.concatenate([shifted[:, :chans], shifted[:, chans:]], 0)
        x[pl.ds(0, 2 * rows), lanes] = jnp.where(mine == 1, column, 0.0).astype(BF16)
        x[pl.ds(2 * rows + height, 2 * rows), lanes] = jnp.where(mine == 0, column, 0.0).astype(BF16)


def convolve(x, wc, wl, wr, b_up, owners, mine, wide, out, rows, cols):
    chans2 = wc.shape[2]
    chans = chans2 // 2
    height = 2 * rows * cols
    lanes = wc.shape[1]
    part = wl.shape[1]
    col_of = lax.broadcasted_iota(jnp.int32, (height, 1), 0) // (2 * rows)
    strip_from = jnp.where(mine == 0, cols - OV, 0)
    soft = 1.0 - 0.5 / (2 * OV)
    scale_l = jnp.where(col_of == strip_from, soft, 1.0)
    scale_r = jnp.where(col_of == strip_from + OV - 1, soft, 1.0)
    bias = jnp.concatenate([b_up[...], b_up[...]], -1)
    for pr in range(2):
        span = pl.ds(pr * chans, chans2)
        mid = dot_t(x[pl.ds(2 * rows, height), span], wc[pr])
        left = dot_t(x[pl.ds(0, height), span], wl[pr]) * scale_l
        right = dot_t(x[pl.ds(4 * rows, height), span], wr[pr]) * scale_r
        low = mid[:, : lanes - part] + left[:, : lanes - part]
        centre = mid[:, lanes - part : part] + left[:, lanes - part :] + right[:, : 2 * part - lanes]
        high = mid[:, part:] + right[:, 2 * part - lanes :]
        y = jnp.concatenate([low, centre, high], -1) + bias
        for col in range(cols):
            for h in range(2):
                top = col * 2 * rows + h * rows
                for j in range(lanes // 128):
                    wide[h, col * lanes // 128 + j, pl.ds(pr, rows, stride=2), :] = y[
                        top : top + rows, j * 128 : (j + 1) * 128
                    ]
    out_row = lax.broadcasted_iota(jnp.int32, (2 * rows, 128), 0)
    keep = jnp.zeros((2 * rows, 128), jnp.int32)
    for r in range(2 * rows):
        keep = jnp.where(out_row == r, owners[r], keep)
    keep = keep == mine
    for col in range(cols):
        shared = col < OV or col >= cols - OV
        outside = (col < strip_from) | (col >= strip_from + OV)
        for h in range(2):
            for lane in range(col * lanes, (col + 1) * lanes, 128):
                block = wide[h, lane // 128]
                if shared:
                    block = jnp.where(keep | outside, block, 0.0)
                out[h, :, pl.ds(lane, 128)] = block.astype(BF16)


def pack_kernel(frame_counts, own, own_far, to_far, to_near):
    slots, rows, cols, chans = own.shape
    pixels = rows * cols
    mine = lax.axis_index("tile")
    two = frame_counts[0] >= 2
    latest = jnp.where(two, own[1].reshape(pixels, chans), own[0].reshape(pixels, chans))
    latest_far = jnp.where(two, own_far[1].reshape(pixels, chans), own_far[0].reshape(pixels, chans))
    theirs = picker(rows, cols, jnp.where(mine == 0, OV, cols - OV - 1))
    edge = picker(rows, cols, jnp.where(mine == 0, cols - OV - 1, OV))
    to_far[pl.ds(0, pixels), :] = latest
    to_far[pl.ds(pixels, 2 * rows), :] = dot(theirs, latest_far).astype(BF16)
    to_near[pl.ds(0, 2 * rows), :] = dot(edge, own[0].reshape(pixels, chans)).astype(BF16)
    to_near[pl.ds(2 * rows, 2 * rows), :] = dot(edge, own[1].reshape(pixels, chans)).astype(BF16)
    mark = jnp.where(two, 2.0, 1.0)
    to_near[pl.ds(4 * rows, 2 * rows), :] = jnp.full((2 * rows, chans), mark, F32).astype(BF16)


def local_kernel(own, own_far, w_time, b_time, w_up, t0, t1, place, wc, wl, wr, lhs):
    slots, rows, cols, chans = own.shape
    pixels = rows * cols
    mine = lax.axis_index("tile")
    pick = picker(rows, cols, jnp.where(mine == 0, OV, cols - OV - 1))
    for k in range(2):
        lhs[k, pl.ds(0, pixels), :] = own[k].reshape(pixels, chans)
        lhs[k, pl.ds(pixels, 2 * rows), :] = dot(pick, own_far[k].reshape(pixels, chans)).astype(BF16)
    t0[...] = b_time[...] + dot(lhs[0], w_time[2])
    t1[...] = b_time[...] + dot(lhs[1], w_time[2]) + dot(lhs[0], w_time[1])
    place[...] = placement(rows, cols)
    prepare_weights(w_up, wc, wl, wr)


def near_is_two(edges, rows):
    return jnp.max(edges[pl.ds(4 * rows, 2 * rows), :].astype(F32)) > 1.5


def near_kernel(
    frame_counts, owners, near, edges, w_time, b_up, t0, t1, place, wc, wl, wr, out, t0_new, lhs, x, wide
):
    slots, rows, cols, chans = near.shape
    pixels = rows * cols
    mine = lax.axis_index("tile")
    first = lax.axis_index("tm") == 0
    two = near_is_two(edges, rows)
    newer = jnp.where(two, near[1].reshape(pixels, chans), near[0].reshape(pixels, chans))
    newer_far = jnp.where(two, edges[pl.ds(2 * rows, 2 * rows), :], edges[pl.ds(0, 2 * rows), :])
    lhs[pl.ds(0, pixels), :] = jnp.where(first, jnp.zeros_like(newer), newer)
    lhs[pl.ds(pixels, 2 * rows), :] = jnp.where(first, jnp.zeros_like(newer_far), newer_far)

    @pl.when(frame_counts[0] >= 2)
    def _():
        t = t1[...] + dot(lhs[...], w_time[0])
        fill_x(t, mine, place, x, rows, cols)
        convolve(x, wc, wl, wr, b_up, owners, mine, wide, out, rows, cols)

    @pl.when(frame_counts[0] < 2)
    def _():
        out[...] = jnp.zeros_like(out)

    t0_new[...] = t0[...] + dot(lhs[...], w_time[1])


def far_kernel(
    owners, near, edges, far, w_time, b_up, t0, place, wc, wl, wr, done, out, lhs, x, wide
):
    slots, rows, cols, chans = near.shape
    pixels = rows * cols
    mine = lax.axis_index("tile")
    place_tm = lax.axis_index("tm")
    two = near_is_two(edges, rows)
    older = jnp.where(two, near[0].reshape(pixels, chans), far[pl.ds(0, pixels), :])
    older_far = jnp.where(two, edges[pl.ds(0, 2 * rows), :], far[pl.ds(pixels, 2 * rows), :])
    none = (place_tm == 0) | ((place_tm == 1) & jnp.logical_not(two))
    lhs[pl.ds(0, pixels), :] = jnp.where(none, jnp.zeros_like(older), older)
    lhs[pl.ds(pixels, 2 * rows), :] = jnp.where(none, jnp.zeros_like(older_far), older_far)
    t = t0[...] + dot(lhs[...], w_time[0])
    fill_x(t, mine, place, x, rows, cols)
    convolve(x, wc, wl, wr, b_up, owners, mine, wide, out, rows, cols)


def per_device(latents, frame_counts, owners, w_time, b_time, w_up, b_up):
    slots, rows, cols, chans = latents.shape
    outc = w_up.shape[3]
    ring = lax.axis_size("tm")
    other = [(0, 1), (1, 0)]
    pixels, extra = rows * cols, 2 * rows
    lanes = 2 * cols * outc
    shape = jax.ShapeDtypeStruct

    def step(k):
        return [(i, (i + k) % ring) for i in range(ring)]

    def step_flip(k):
        return [(2 * i + t, 2 * ((i + k) % ring) + 1 - t) for i in range(ring) for t in range(2)]

    w_up = w_up.transpose(0, 1, 3, 2)
    b_time = b_time.reshape(1, -1)
    b_up = b_up.reshape(1, -1)
    near = lax.ppermute(latents, "tm", step(1))
    own_far = lax.ppermute(latents, "tile", other)
    to_far, to_near = pl.pallas_call(
        pack_kernel,
        out_shape=(shape((pixels + extra, chans), BF16), shape((3 * extra, chans), BF16)),
        in_specs=[SMEM, VMEM, VMEM],
        out_specs=(VMEM, VMEM),
        compiler_params=PARAMS,
        cost_estimate=cost(10**7, 600_000),
        name="pack",
    )(frame_counts, latents, own_far)
    far = lax.ppermute(to_far, "tm", step(2))
    edges = lax.ppermute(to_near, ("tm", "tile"), step_flip(1))
    partial = shape((pixels + extra, 2 * chans), F32)
    x_shape = pltpu.VMEM(((cols + 2) * extra, 3 * chans), BF16)
    wide_shape = pltpu.VMEM((2, lanes // 128, extra, 128), F32)
    t0, t1, place, wc, wl, wr = pl.pallas_call(
        local_kernel,
        out_shape=(
            partial,
            partial,
            shape((6 * pixels, 2 * pixels), BF16),
            shape((2, 2 * outc, 2 * chans), BF16),
            shape((2, 256, 2 * chans), BF16),
            shape((2, 256, 2 * chans), BF16),
        ),
        in_specs=[VMEM] * 5,
        out_specs=(VMEM,) * 6,
        scratch_shapes=[pltpu.VMEM((2, pixels + extra, chans), BF16)],
        compiler_params=PARAMS,
        cost_estimate=cost(6 * 10**8, 6 << 20),
        name="local",
    )(latents, own_far, w_time, b_time, w_up)
    out, t0 = pl.pallas_call(
        near_kernel,
        grid=(1,),
        out_shape=(shape((2 * slots, 2 * rows, lanes), BF16), partial),
        in_specs=[SMEM, SMEM] + [VMEM] * 10,
        out_specs=(pl.BlockSpec((2, 2 * rows, lanes), lambda i: (1, 0, 0)), VMEM),
        scratch_shapes=[pltpu.VMEM((pixels + extra, chans), BF16), x_shape, wide_shape],
        compiler_params=PARAMS,
        cost_estimate=cost(10**9, 4 << 20),
        name="near",
    )(frame_counts, owners, near, edges, w_time, b_up, t0, t1, place, wc, wl, wr)
    return pl.pallas_call(
        far_kernel,
        grid=(1,),
        out_shape=shape((2 * slots, 2 * rows, lanes), BF16),
        in_specs=[SMEM] + [VMEM] * 10 + [ANY],
        out_specs=pl.BlockSpec((2, 2 * rows, lanes), lambda i: (0, 0, 0)),
        scratch_shapes=[pltpu.VMEM((pixels + extra, chans), BF16), x_shape, wide_shape],
        input_output_aliases={11: 0},
        compiler_params=PARAMS,
        cost_estimate=cost(10**9, 4 << 20),
        name="far",
    )(owners, near, edges, far, w_time, b_up, t0, place, wc, wl, wr, out)


def solution(mesh):
    placed = (
        P(("videos", "tm"), None, "tile", None),
        P(("videos", "tm")),
        P("videos"),
        P(),
        P(),
        P(),
        P(),
    )
    return jax.shard_map(
        per_device,
        mesh=mesh,
        in_specs=placed,
        out_specs=P(("videos", "tm"), None, "tile"),
        check_vma=False,
    )
```

time: 26.7 us -> 19.1 us (0.72)
  waiting for transfers between devices: 8.32 us -> 0.01 us
  Pallas kernels: 5.93 us -> 7.8 us
  local copies, waits for them, and re-layouts: 5.6 us -> 4.43 us
  starting transfers between devices: 5.2 us -> 5.93 us
  other arithmetic: 0.7 us -> 0 us
    ppermute x1, waiting for transfers between devices: 5.79 us -> 0.01 us  [per_device(): near = lax.ppermute(latents, 'tm', step(1))]
    ppermute x4 -> x2, waiting for transfers between devices: 2.53 us -> 0.01 us  [the longest x1 0.01 us: per_device(): edges = lax.ppermute(to_near, ('tm', 'tile'), step_flip(1))]
    pallas_call x1 -> x4, Pallas kernels: 5.93 us -> 7.8 us  [the longest x1 3.04 us: per_device(): pl.pallas_call(near_kernel, grid=(1,), out_shape=(shape((2 * slots, 2 * r...]
    dynamic_slice x1 -> x0, local copies, waits for them, and re-layouts: 0.91 us -> none  [per_device(): latest = lax.dynamic_slice_in_dim(latents, count - 1, 1, 0)]
    ppermute x4 -> x2, starting transfers between devices: 2.21 us -> 2.99 us  [the longest x1 1.58 us: per_device(): far = lax.ppermute(to_far, 'tm', step(2))]
    another operation x1 -> x0, other arithmetic: 0.7 us -> none  [per_device(): facts = jnp.stack([mine, count, count_near[0], place_tm]).astype(jnp.int32)]
    ppermute x1, starting transfers between devices: 2.99 us -> 2.49 us  [per_device(): near = lax.ppermute(latents, 'tm', step(1))]
    ppermute x1, starting transfers between devices: 0.01 us -> 0.45 us  [per_device(): own_far = lax.ppermute(latents, 'tile', other)]
  transfers between devices with their start and end apart: 6 -> 4, of which waited for: 2 -> 0; matrix products, arithmetic and copies ran while one was open for 18% -> 4% of each run, Pallas kernels for 0% -> 26%
where the time goes in v2:
time: 19.1 us; the launch traced here: 18.9 us
  Pallas kernels  7.8 us (41%)
  starting transfers between devices  5.93 us (31%)
  local copies, waits for them, and re-layouts  4.43 us (23%)
  between operations  0.71 us (4%)
    unnamed x12, local copies, waits for them, and re-layouts  3.74 us
    pallas_call x1, Pallas kernels, per_device(): pl.pallas_call(near_kernel, grid=(1,), out_shape=(shape((2 * slots, 2 * r...  3.04 us
    pallas_call x1, Pallas kernels, per_device(): pl.pallas_call(far_kernel, grid=(1,), out_shape=shape((2 * slots, 2 * row...  2.98 us
    ppermute x1, starting transfers between devices, per_device(): near = lax.ppermute(latents, 'tm', step(1))  2.49 us
    pallas_call x1, Pallas kernels, per_device(): pl.pallas_call(local_kernel, out_shape=(partial, partial, shape((6 * pixe...  1.61 us
    ppermute x1, starting transfers between devices, per_device(): far = lax.ppermute(to_far, 'tm', step(2))  1.58 us
    ppermute x1, starting transfers between devices, per_device(): edges = lax.ppermute(to_near, ('tm', 'tile'), step_flip(1))  1.41 us
    reshape x1, local copies, waits for them, and re-layouts, per_device(): b_time = b_time.reshape(1, -1)  0.69 us
  transfers between devices with their start and end apart: 4, of which 0 were waited for; matrix products, arithmetic and copies ran while one was open for 4% of the time, Pallas kernels for 26%

profile of v2, /device:TPU:0, one launch (start us, length us, event | category | flops | bytes accessed | tf_op | source)
XLA Modules:
  0.0 18.9 jit_solution(16055056670909987771)
XLA Ops:
  0.0 0.5 %collective-permute-start.1 = (bf16[2,8,16,384]{3,2,1,0:T(8,128)(2,1)}, bf16[2,8,16,384]{3,2,1,0:T(8,128)(2,1)S(1)}, u32[]{:S(2)}, u32[]{:S(2)}) collective-permute-start(bf16[2,8,16,384]{3,2,1,0:T(8,128)(2,1)} %own.3), channel_id=1, source_target_pairs={{0,1},{1,0},{2,3},{3,2},{4,5},{5,4},{6,7},{7,6},{8,9},{9,8},{10,11... | collective-permute-start | bytes 589832 | tf_op jit(solution)/shard_map/ppermute | solution.py:231
  0.5 2.5 %collective-permute-start = (bf16[2,8,16,384]{3,2,1,0:T(8,128)(2,1)}, bf16[2,8,16,384]{3,2,1,0:T(8,128)(2,1)S(1)}, u32[]{:S(2)}, u32[]{:S(2)}) collective-permute-start(bf16[2,8,16,384]{3,2,1,0:T(8,128)(2,1)} %own.3), channel_id=1, source_target_pairs={{0,2},{2,4},{4,6},{6,8},{8,10},{10,12},{12,14},{14,0},{1,3},{3,5},... | collective-permute-start | bytes 589832 | tf_op jit(solution)/shard_map/ppermute | solution.py:230
  3.6 0.7 %reshape.7.b_time = f32[1,768]{1,0:T(1,128)S(1)} reshape(f32[768]{0:T(1024)} %param.11) | data formatting | bytes 6144 | tf_op jit(solution)/shard_map/reshape | solution.py:228
  4.3 0.0 collective-permute-done.1.own_far
  4.3 0.0 copy-start.3
  4.3 0.9 %copy-done.3 = bf16[2,8,16,384]{3,2,1,0:T(8,128)(2,1)S(1)} copy-done((bf16[2,8,16,384]{3,2,1,0:T(8,128)(2,1)S(1)}, bf16[2,8,16,384]{3,2,1,0:T(8,128)(2,1)}, u32[]{:S(2)}) %copy-start.3) | copy-done | bytes 196632
  5.2 0.2 pack.1
  5.4 1.4 %collective-permute-start.2 = (bf16[48,384]{1,0:T(8,128)(2,1)S(1)}, bf16[48,384]{1,0:T(8,128)(2,1)S(1)}, u32[]{:S(2)}, u32[]{:S(2)}) collective-permute-start(bf16[48,384]{1,0:T(8,128)(2,1)S(1)} %get-tuple-element.15), channel_id=1, source_target_pairs={{0,3},{1,2},{2,5},{3,4},{4,7},{5,6},{6,9},{7,8},{8,11},{9,10},{10,... | collective-permute-start | bytes 110600 | tf_op jit(solution)/shard_map/ppermute | solution.py:242
  6.8 1.6 %collective-permute-start.3 = (bf16[144,384]{1,0:T(8,128)(2,1)S(1)}, bf16[144,384]{1,0:T(8,128)(2,1)S(1)}, u32[]{:S(2)}, u32[]{:S(2)}) collective-permute-start(bf16[144,384]{1,0:T(8,128)(2,1)S(1)} %get-tuple-element.16), channel_id=1, source_target_pairs={{0,4},{2,6},{4,8},{6,10},{8,12},{10,14},{12,0},{14,2},{1,5},{3,7},... | collective-permute-start | bytes 331784 | tf_op jit(solution)/shard_map/ppermute | solution.py:241
  8.4 0.0 copy-start
  8.4 1.5 %copy-done = bf16[3,384,768]{2,1,0:T(8,128)(2,1)S(1)} copy-done((bf16[3,384,768]{2,1,0:T(8,128)(2,1)S(1)}, bf16[3,384,768]{2,1,0:T(8,128)(2,1)}, u32[]{:S(2)}) %copy-start) | copy-done | bytes 1769496
  9.9 0.0 copy-start.2
  9.9 1.3 %copy-done.2 = bf16[3,3,384,192]{2,3,1,0:T(8,128)(2,1)S(1)} copy-done((bf16[3,3,384,192]{2,3,1,0:T(8,128)(2,1)S(1)}, bf16[3,3,384,192]{2,3,1,0:T(8,128)(2,1)}, u32[]{:S(2)}) %copy-start.2) | copy-done | bytes 1327128
  11.2 0.0 copy-start.1
  11.2 0.0 copy-start.4
  11.2 1.6 %local.1 = (f32[144,768]{1,0:T(8,128)S(1)}, f32[144,768]{1,0:T(8,128)S(1)}, bf16[768,256]{1,0:T(8,128)(2,1)S(1)}, bf16[2,384,768]{2,1,0:T(8,128)(2,1)S(1)}, bf16...) custom-call(bf16[2,8,16,384]{3,2,1,0:T(8,128)(2,1)S(1)} %copy-done.3, ...), custom_call_target="tpu_custom_call" | custom-call | flops 600000000 | bytes 6291456 | tf_op jit(solution)/shard_map/local/pallas_call | solution.py:246
  12.8 0.0 collective-permute-done.near
  12.8 0.0 collective-permute-done.2.edges
  12.8 0.0 copy-done.1
  12.8 0.0 copy-done.4
  12.8 0.0 copy-done.5
  12.9 3.0 %near.1 = (bf16[4,16,6144]{2,1,0:T(8,128)(2,1)}, f32[144,768]{1,0:T(8,128)S(1)}) custom-call(s32[1]{0:T(128)S(6)} %copy.10.frame_counts, s32[16]{0:T(128)S(1)} %copy-done.5, bf16[2,8,16,384]{3,2,1,0:T(8,128)(2,1)S(1)} %collective-permute-done.near, bf16[48,384]{1,0:T(8,128)(2,1)S(1)} %collective-permute-done.2.edges, bf16[3,384,768]{2,1,0:T(8,128)(2,1)S(1)} %copy-done.1, ...), custom_call_target="tpu_custom_call" | custom-call | flops 1000000000 | bytes 4194304 | tf_op jit(solution)/shard_map/near/pallas_call | solution.py:263
  15.9 0.0 collective-permute-done.3.far
  15.9 3.0 %far.1 = bf16[4,16,6144]{2,1,0:T(8,128)(2,1)} custom-call(s32[16]{0:T(128)S(1)} %copy-done.5, bf16[2,8,16,384]{3,2,1,0:T(8,128)(2,1)S(1)} %collective-permute-done.near, bf16[48,384]{1,0:T(8,128)(2,1)S(1)} %collective-permute-done.2.edges, bf16[144,384]{1,0:T(8,128)(2,1)S(1)} %collective-permute-done.3.far, ...), custom_call_target="tpu_custom_call", output_to_operand_aliasing={{}: (11, {})} | custom-call | flops 1000000000 | bytes 4194304 | tf_op jit(solution)/shard_map/far/pallas_call | solution.py:274
  (1 shorter events, 0.0 us)
Async XLA Ops:
  0.0 4.3 %collective-permute-start.1 = (bf16[2,8,16,384]{3,2,1,0:T(8,128)(2,1)}, bf16[2,8,16,384]{3,2,1,0:T(8,128)(2,1)S(1)}, u32[]{:S(2)}, u32[]{:S(2)}) collective-permute-start(bf16[2,8,16,384]{3,2,1,0:T(8,128)(2,1)} %own.3), channel_id=1, source_target_pairs={{0,1},{1,0},{2,3},{3,2},{4,5},{5,4},{6,7},{7,6},{8,9},{9,8},{10,11... | collective-permute-start | bytes 589832 | tf_op jit(solution)/shard_map/ppermute | solution.py:231
  0.5 12.4 %collective-permute-start = (bf16[2,8,16,384]{3,2,1,0:T(8,128)(2,1)}, bf16[2,8,16,384]{3,2,1,0:T(8,128)(2,1)S(1)}, u32[]{:S(2)}, u32[]{:S(2)}) collective-permute-start(bf16[2,8,16,384]{3,2,1,0:T(8,128)(2,1)} %own.3), channel_id=1, source_target_pairs={{0,2},{2,4},{4,6},{6,8},{8,10},{10,12},{12,14},{14,0},{1,3},{3,5},... | collective-permute-start | bytes 589832 | tf_op jit(solution)/shard_map/ppermute | solution.py:230
  4.3 0.9 %copy-start.3 = (bf16[2,8,16,384]{3,2,1,0:T(8,128)(2,1)S(1)}, bf16[2,8,16,384]{3,2,1,0:T(8,128)(2,1)}, u32[]{:S(2)}) copy-start(bf16[2,8,16,384]{3,2,1,0:T(8,128)(2,1)} %own.3) | copy-start | bytes 589828
  5.4 7.4 %collective-permute-start.2 = (bf16[48,384]{1,0:T(8,128)(2,1)S(1)}, bf16[48,384]{1,0:T(8,128)(2,1)S(1)}, u32[]{:S(2)}, u32[]{:S(2)}) collective-permute-start(bf16[48,384]{1,0:T(8,128)(2,1)S(1)} %get-tuple-element.15), channel_id=1, source_target_pairs={{0,3},{1,2},{2,5},{3,4},{4,7},{5,6},{6,9},{7,8},{8,11},{9,10},{10,... | collective-permute-start | bytes 110600 | tf_op jit(solution)/shard_map/ppermute | solution.py:242
  6.8 9.1 %collective-permute-start.3 = (bf16[144,384]{1,0:T(8,128)(2,1)S(1)}, bf16[144,384]{1,0:T(8,128)(2,1)S(1)}, u32[]{:S(2)}, u32[]{:S(2)}) collective-permute-start(bf16[144,384]{1,0:T(8,128)(2,1)S(1)} %get-tuple-element.16), channel_id=1, source_target_pairs={{0,4},{2,6},{4,8},{6,10},{8,12},{10,14},{12,0},{14,2},{1,5},{3,7},... | collective-permute-start | bytes 331784 | tf_op jit(solution)/shard_map/ppermute | solution.py:241
  8.4 1.5 %copy-start = (bf16[3,384,768]{2,1,0:T(8,128)(2,1)S(1)}, bf16[3,384,768]{2,1,0:T(8,128)(2,1)}, u32[]{:S(2)}) copy-start(bf16[3,384,768]{2,1,0:T(8,128)(2,1)} %w_time.5) | copy-start | bytes 5308420
  9.9 1.3 %copy-start.2 = (bf16[3,3,384,192]{2,3,1,0:T(8,128)(2,1)S(1)}, bf16[3,3,384,192]{2,3,1,0:T(8,128)(2,1)}, u32[]{:S(2)}) copy-start(bf16[3,3,384,192]{2,3,1,0:T(8,128)(2,1)} %param.12) | copy-start | bytes 3981316
  11.2 1.6 %copy-start.1 = (bf16[3,384,768]{2,1,0:T(8,128)(2,1)S(1)}, bf16[3,384,768]{2,1,0:T(8,128)(2,1)}, u32[]{:S(2)}) copy-start(bf16[3,384,768]{2,1,0:T(8,128)(2,1)} %w_time.5) | copy-start | bytes 5308420
  11.2 1.7 %copy-start.4 = (f32[192]{0:T(256)S(1)}, f32[192]{0:T(256)}, u32[]{:S(2)}) copy-start(f32[192]{0:T(256)} %param.13) | copy-start | bytes 2308
  11.2 1.7 %copy-start.5 = (s32[16]{0:T(128)S(1)}, s32[16]{0:T(128)}, u32[]{:S(2)}) copy-start(s32[16]{0:T(128)} %owners.3) | copy-start | bytes 196

commit v3 on v2

--- a/solution.py
+++ b/solution.py
@@ -10,7 +10,8 @@
 BF16 = jnp.bfloat16
 VMEM = pl.BlockSpec(memory_space=pltpu.VMEM)
 SMEM = pl.BlockSpec(memory_space=pltpu.SMEM)
-ANY = pl.BlockSpec(memory_space=pl.ANY)
+HBM = pl.BlockSpec(memory_space=pltpu.HBM)
+LEAVES = 4
 PARAMS = pltpu.CompilerParams(vmem_limit_bytes=24 << 20)
 
 
@@ -86,7 +87,7 @@
         x[pl.ds(2 * rows + height, 2 * rows), lanes] = jnp.where(mine == 0, column, 0.0).astype(BF16)
 
 
-def convolve(x, wc, wl, wr, b_up, owners, mine, wide, out, rows, cols):
+def convolve(x, wc, wl, wr, b_up, keep, mine, wide, done, out, sems, rows, cols):
     chans2 = wc.shape[2]
     chans = chans2 // 2
     height = 2 * rows * cols
@@ -97,7 +98,8 @@
     soft = 1.0 - 0.5 / (2 * OV)
     scale_l = jnp.where(col_of == strip_from, soft, 1.0)
     scale_r = jnp.where(col_of == strip_from + OV - 1, soft, 1.0)
-    bias = jnp.concatenate([b_up[...], b_up[...]], -1)
+    bias = b_up[...].reshape(1, -1)
+    bias = jnp.concatenate([bias, bias], -1)
     for pr in range(2):
         span = pl.ds(pr * chans, chans2)
         mid = dot_t(x[pl.ds(2 * rows, height), span], wc[pr])
@@ -114,11 +116,8 @@
                     wide[h, col * lanes // 128 + j, pl.ds(pr, rows, stride=2), :] = y[
                         top : top + rows, j * 128 : (j + 1) * 128
                     ]
-    out_row = lax.broadcasted_iota(jnp.int32, (2 * rows, 128), 0)
-    keep = jnp.zeros((2 * rows, 128), jnp.int32)
-    for r in range(2 * rows):
-        keep = jnp.where(out_row == r, owners[r], keep)
-    keep = keep == mine
+    keep = keep[...] > 0.5
+    copies = leave(done, out, sems)
     for col in range(cols):
         shared = col < OV or col >= cols - OV
         outside = (col < strip_from) | (col >= strip_from + OV)
@@ -127,24 +126,57 @@
                 block = wide[h, lane // 128]
                 if shared:
                     block = jnp.where(keep | outside, block, 0.0)
-                out[h, :, pl.ds(lane, 128)] = block.astype(BF16)
-
-
-def pack_kernel(frame_counts, own, own_far, to_far, to_near):
+                done[h, :, pl.ds(lane, 128)] = block.astype(BF16)
+        if (col + 1) % (cols // LEAVES) == 0:
+            copies[col // (cols // LEAVES)].start()
+
+
+def leave(done, out, sems):
+    width = done.shape[2] // LEAVES
+    spans = [pl.ds(k * width, width) for k in range(LEAVES)]
+    return [
+        pltpu.make_async_copy(done.at[:, :, span], out.at[:, :, span], sems.at[k])
+        for k, span in enumerate(spans)
+    ]
+
+
+def pack_kernel(
+    counts, owners_hbm, own_hbm, own_far, w_time_hbm, w_up_hbm,
+    to_far, to_near, keep, own, w_time, w_up, owners, sems,
+):
+    loads = [
+        pltpu.make_async_copy(source, target, sems.at[k])
+        for k, (source, target) in enumerate(
+            [(own_hbm, own), (owners_hbm, owners)]
+            + [(w_time_hbm.at[2 - k], w_time.at[2 - k]) for k in range(3)]
+            + [(w_up_hbm.at[k], w_up.at[k]) for k in range(3)]
+        )
+    ]
+    for load in loads:
+        load.start()
     slots, rows, cols, chans = own.shape
     pixels = rows * cols
     mine = lax.axis_index("tile")
-    two = frame_counts[0] >= 2
+    theirs = picker(rows, cols, jnp.where(mine == 0, OV, cols - OV - 1))
+    edge = picker(rows, cols, jnp.where(mine == 0, cols - OV - 1, OV))
+    for load in loads[:2]:
+        load.wait()
+    two = counts[0] >= 2
     latest = jnp.where(two, own[1].reshape(pixels, chans), own[0].reshape(pixels, chans))
     latest_far = jnp.where(two, own_far[1].reshape(pixels, chans), own_far[0].reshape(pixels, chans))
-    theirs = picker(rows, cols, jnp.where(mine == 0, OV, cols - OV - 1))
-    edge = picker(rows, cols, jnp.where(mine == 0, cols - OV - 1, OV))
     to_far[pl.ds(0, pixels), :] = latest
     to_far[pl.ds(pixels, 2 * rows), :] = dot(theirs, latest_far).astype(BF16)
     to_near[pl.ds(0, 2 * rows), :] = dot(edge, own[0].reshape(pixels, chans)).astype(BF16)
     to_near[pl.ds(2 * rows, 2 * rows), :] = dot(edge, own[1].reshape(pixels, chans)).astype(BF16)
     mark = jnp.where(two, 2.0, 1.0)
     to_near[pl.ds(4 * rows, 2 * rows), :] = jnp.full((2 * rows, chans), mark, F32).astype(BF16)
+    out_row = lax.broadcasted_iota(jnp.int32, keep.shape, 0)
+    owner = jnp.zeros(keep.shape, jnp.int32)
+    for r in range(2 * rows):
+        owner = jnp.where(out_row == r, owners[r], owner)
+    keep[...] = jnp.where(owner == mine, 1.0, 0.0)
+    for load in loads[2:]:
+        load.wait()
 
 
 def local_kernel(own, own_far, w_time, b_time, w_up, t0, t1, place, wc, wl, wr, lhs):
@@ -155,50 +187,56 @@
     for k in range(2):
         lhs[k, pl.ds(0, pixels), :] = own[k].reshape(pixels, chans)
         lhs[k, pl.ds(pixels, 2 * rows), :] = dot(pick, own_far[k].reshape(pixels, chans)).astype(BF16)
-    t0[...] = b_time[...] + dot(lhs[0], w_time[2])
-    t1[...] = b_time[...] + dot(lhs[1], w_time[2]) + dot(lhs[0], w_time[1])
+    bias = b_time[...].reshape(1, -1)
+    t0[...] = bias + dot(lhs[0], w_time[2])
+    t1[...] = bias + dot(lhs[1], w_time[2]) + dot(lhs[0], w_time[1])
     place[...] = placement(rows, cols)
     prepare_weights(w_up, wc, wl, wr)
 
 
-def near_is_two(edges, rows):
-    return jnp.max(edges[pl.ds(4 * rows, 2 * rows), :].astype(F32)) > 1.5
+def is_two(marks, rows):
+    return jnp.max(marks[pl.ds(4 * rows, 2 * rows), :].astype(F32)) > 1.5
 
 
 def near_kernel(
-    frame_counts, owners, near, edges, w_time, b_up, t0, t1, place, wc, wl, wr, out, t0_new, lhs, x, wide
+    marks, keep, near, edges, w_time, b_up, t0, t1, place, wc, wl, wr, out, t0_new, lhs, x, wide, done, sems
 ):
     slots, rows, cols, chans = near.shape
     pixels = rows * cols
     mine = lax.axis_index("tile")
     first = lax.axis_index("tm") == 0
-    two = near_is_two(edges, rows)
+    two = is_two(edges, rows)
     newer = jnp.where(two, near[1].reshape(pixels, chans), near[0].reshape(pixels, chans))
     newer_far = jnp.where(two, edges[pl.ds(2 * rows, 2 * rows), :], edges[pl.ds(0, 2 * rows), :])
     lhs[pl.ds(0, pixels), :] = jnp.where(first, jnp.zeros_like(newer), newer)
     lhs[pl.ds(pixels, 2 * rows), :] = jnp.where(first, jnp.zeros_like(newer_far), newer_far)
-
-    @pl.when(frame_counts[0] >= 2)
+    valid = is_two(marks, rows)
+
+    @pl.when(valid)
     def _():
         t = t1[...] + dot(lhs[...], w_time[0])
         fill_x(t, mine, place, x, rows, cols)
-        convolve(x, wc, wl, wr, b_up, owners, mine, wide, out, rows, cols)
-
-    @pl.when(frame_counts[0] < 2)
+        convolve(x, wc, wl, wr, b_up, keep, mine, wide, done, out.at[pl.ds(2, 2)], sems, rows, cols)
+
+    @pl.when(jnp.logical_not(valid))
     def _():
-        out[...] = jnp.zeros_like(out)
+        done[...] = jnp.zeros_like(done)
+        for copy in leave(done, out.at[pl.ds(2, 2)], sems):
+            copy.start()
 
     t0_new[...] = t0[...] + dot(lhs[...], w_time[1])
+    for copy in leave(done, out.at[pl.ds(2, 2)], sems):
+        copy.wait()
 
 
 def far_kernel(
-    owners, near, edges, far, w_time, b_up, t0, place, wc, wl, wr, done, out, lhs, x, wide
+    keep, near, edges, far, w_time, b_up, t0, place, wc, wl, wr, before, out, lhs, x, wide, done, sems
 ):
     slots, rows, cols, chans = near.shape
     pixels = rows * cols
     mine = lax.axis_index("tile")
     place_tm = lax.axis_index("tm")
-    two = near_is_two(edges, rows)
+    two = is_two(edges, rows)
     older = jnp.where(two, near[0].reshape(pixels, chans), far[pl.ds(0, pixels), :])
     older_far = jnp.where(two, edges[pl.ds(0, 2 * rows), :], far[pl.ds(pixels, 2 * rows), :])
     none = (place_tm == 0) | ((place_tm == 1) & jnp.logical_not(two))
@@ -206,7 +244,9 @@
     lhs[pl.ds(pixels, 2 * rows), :] = jnp.where(none, jnp.zeros_like(older_far), older_far)
     t = t0[...] + dot(lhs[...], w_time[0])
     fill_x(t, mine, place, x, rows, cols)
-    convolve(x, wc, wl, wr, b_up, owners, mine, wide, out, rows, cols)
+    convolve(x, wc, wl, wr, b_up, keep, mine, wide, done, out.at[pl.ds(0, 2)], sems, rows, cols)
+    for copy in leave(done, out.at[pl.ds(0, 2)], sems):
+        copy.wait()
 
 
 def per_device(latents, frame_counts, owners, w_time, b_time, w_up, b_up):
@@ -224,25 +264,42 @@
     def step_flip(k):
         return [(2 * i + t, 2 * ((i + k) % ring) + 1 - t) for i in range(ring) for t in range(2)]
 
+    def stay(v):
+        return pltpu.with_memory_space_constraint(v, pltpu.HBM)
+
     w_up = w_up.transpose(0, 1, 3, 2)
-    b_time = b_time.reshape(1, -1)
-    b_up = b_up.reshape(1, -1)
     near = lax.ppermute(latents, "tm", step(1))
     own_far = lax.ppermute(latents, "tile", other)
-    to_far, to_near = pl.pallas_call(
+    to_far, to_near, keep, own, w_time, w_up = pl.pallas_call(
         pack_kernel,
-        out_shape=(shape((pixels + extra, chans), BF16), shape((3 * extra, chans), BF16)),
-        in_specs=[SMEM, VMEM, VMEM],
-        out_specs=(VMEM, VMEM),
+        out_shape=(
+            shape((pixels + extra, chans), BF16),
+            shape((3 * extra, chans), BF16),
+            shape((extra, 128), F32),
+            shape(latents.shape, BF16),
+            shape(w_time.shape, BF16),
+            shape(w_up.shape, BF16),
+        ),
+        in_specs=[SMEM, HBM, HBM, VMEM, HBM, HBM],
+        out_specs=(VMEM,) * 6,
+        scratch_shapes=[
+            pltpu.SMEM(owners.shape, jnp.int32),
+            pltpu.SemaphoreType.DMA((8,)),
+        ],
         compiler_params=PARAMS,
-        cost_estimate=cost(10**7, 600_000),
+        cost_estimate=cost(10**7, 4 << 20),
         name="pack",
-    )(frame_counts, latents, own_far)
+    )(frame_counts, stay(owners), stay(latents), own_far, stay(w_time), stay(w_up))
     far = lax.ppermute(to_far, "tm", step(2))
     edges = lax.ppermute(to_near, ("tm", "tile"), step_flip(1))
     partial = shape((pixels + extra, 2 * chans), F32)
-    x_shape = pltpu.VMEM(((cols + 2) * extra, 3 * chans), BF16)
-    wide_shape = pltpu.VMEM((2, lanes // 128, extra, 128), F32)
+    scratch = [
+        pltpu.VMEM((pixels + extra, chans), BF16),
+        pltpu.VMEM(((cols + 2) * extra, 3 * chans), BF16),
+        pltpu.VMEM((2, lanes // 128, extra, 128), F32),
+        pltpu.VMEM((2, extra, lanes), BF16),
+        pltpu.SemaphoreType.DMA((LEAVES,)),
+    ]
     t0, t1, place, wc, wl, wr = pl.pallas_call(
         local_kernel,
         out_shape=(
@@ -259,30 +316,28 @@
         compiler_params=PARAMS,
         cost_estimate=cost(6 * 10**8, 6 << 20),
         name="local",
-    )(latents, own_far, w_time, b_time, w_up)
+    )(own, own_far, w_time, b_time, w_up)
     out, t0 = pl.pallas_call(
         near_kernel,
-        grid=(1,),
         out_shape=(shape((2 * slots, 2 * rows, lanes), BF16), partial),
-        in_specs=[SMEM, SMEM] + [VMEM] * 10,
-        out_specs=(pl.BlockSpec((2, 2 * rows, lanes), lambda i: (1, 0, 0)), VMEM),
-        scratch_shapes=[pltpu.VMEM((pixels + extra, chans), BF16), x_shape, wide_shape],
+        in_specs=[VMEM] * 12,
+        out_specs=(HBM, VMEM),
+        scratch_shapes=scratch,
         compiler_params=PARAMS,
         cost_estimate=cost(10**9, 4 << 20),
         name="near",
-    )(frame_counts, owners, near, edges, w_time, b_up, t0, t1, place, wc, wl, wr)
+    )(to_near, keep, near, edges, w_time, b_up, t0, t1, place, wc, wl, wr)
     return pl.pallas_call(
         far_kernel,
-        grid=(1,),
         out_shape=shape((2 * slots, 2 * rows, lanes), BF16),
-        in_specs=[SMEM] + [VMEM] * 10 + [ANY],
-        out_specs=pl.BlockSpec((2, 2 * rows, lanes), lambda i: (0, 0, 0)),
-        scratch_shapes=[pltpu.VMEM((pixels + extra, chans), BF16), x_shape, wide_shape],
+        in_specs=[VMEM] * 11 + [HBM],
+        out_specs=HBM,
+        scratch_shapes=scratch,
         input_output_aliases={11: 0},
         compiler_params=PARAMS,
         cost_estimate=cost(10**9, 4 << 20),
         name="far",
-    )(owners, near, edges, far, w_time, b_up, t0, place, wc, wl, wr, out)
+    )(keep, near, edges, far, w_time, b_up, t0, place, wc, wl, wr, out)
 
 
 def solution(mesh):

time: 19.1 us -> 17.3 us (0.906)
  local copies, waits for them, and re-layouts: 4.43 us -> 0.01 us
  waiting for transfers between devices: 0.01 us -> 2.09 us
  Pallas kernels: 7.8 us -> 8.4 us
    unnamed x12 -> x4, local copies, waits for them, and re-layouts: 3.74 us -> 0.01 us
    pallas_call x1, Pallas kernels: 0.17 us -> 1.99 us  [per_device(): pl.pallas_call(pack_kernel, out_shape=(shape((pixels + extra, chans), BF1...]
    ppermute x1, waiting for transfers between devices: 0.01 us -> 1.67 us  [per_device(): near = lax.ppermute(latents, 'tm', step(1))]
    pallas_call x2, Pallas kernels: 6.02 us -> 4.77 us  [the longest x1 2.4 us: per_device(): pl.pallas_call(near_kernel, out_shape=(shape((2 * slots, 2 * rows, lanes)...]
    reshape x1 -> x0, local copies, waits for them, and re-layouts: 0.69 us -> none  [per_device(): b_time = b_time.reshape(1, -1)]
    ppermute x1, waiting for transfers between devices: 0.01 us -> 0.42 us  [per_device(): edges = lax.ppermute(to_near, ('tm', 'tile'), step_flip(1))]
  transfers between devices with their start and end apart: 4 -> 4, of which waited for: 0 -> 2; matrix products, arithmetic and copies ran while one was open for 4% -> 0% of each run, Pallas kernels for 26% -> 35%
where the time goes in v3:
time: 17.3 us; the launch traced here: 17.2 us
  Pallas kernels  8.4 us (49%)
  starting transfers between devices  5.95 us (34%)
  waiting for transfers between devices  2.09 us (12%)
  between operations  0.7 us (4%)
    ppermute x1, starting transfers between devices, per_device(): near = lax.ppermute(latents, 'tm', step(1))  2.49 us
    pallas_call x1, Pallas kernels, per_device(): pl.pallas_call(near_kernel, out_shape=(shape((2 * slots, 2 * rows, lanes)...  2.4 us
    pallas_call x1, Pallas kernels, per_device(): pl.pallas_call(far_kernel, out_shape=shape((2 * slots, 2 * rows, lanes),...  2.37 us
    pallas_call x1, Pallas kernels, per_device(): pl.pallas_call(pack_kernel, out_shape=(shape((pixels + extra, chans), BF1...  1.99 us
    ppermute x1, waiting for transfers between devices, per_device(): near = lax.ppermute(latents, 'tm', step(1))  1.67 us
    pallas_call x1, Pallas kernels, per_device(): pl.pallas_call(local_kernel, out_shape=(partial, partial, shape((6 * pixe...  1.64 us
    ppermute x1, starting transfers between devices, per_device(): far = lax.ppermute(to_far, 'tm', step(2))  1.58 us
    ppermute x1, starting transfers between devices, per_device(): edges = lax.ppermute(to_near, ('tm', 'tile'), step_flip(1))  1.43 us
  transfers between devices with their start and end apart: 4, of which 2 were waited for; matrix products, arithmetic and copies ran while one was open for 0% of the time, Pallas kernels for 35%

profile of v3, /device:TPU:0, one launch (start us, length us, event | category | flops | bytes accessed | tf_op | source)
XLA Modules:
  0.0 17.2 jit_solution(5467538414904776077)
XLA Ops:
  0.0 0.5 %collective-permute-start = (bf16[2,8,16,384]{3,2,1,0:T(8,128)(2,1)}, bf16[2,8,16,384]{3,2,1,0:T(8,128)(2,1)S(1)}, u32[]{:S(2)}, u32[]{:S(2)}) collective-permute-start(bf16[2,8,16,384]{3,2,1,0:T(8,128)(2,1)} %own_hbm.1), channel_id=1, source_target_pairs={{0,1},{1,0},{2,3},{3,2},{4,5},{5,4},{6,7},{7,6},{8,9},{9,8},{10,11... | collective-permute-start | bytes 589832 | tf_op jit(solution)/shard_map/ppermute | solution.py:272
  0.5 2.5 %collective-permute-start.1 = (bf16[2,8,16,384]{3,2,1,0:T(8,128)(2,1)}, bf16[2,8,16,384]{3,2,1,0:T(8,128)(2,1)S(1)}, u32[]{:S(2)}, u32[]{:S(2)}) collective-permute-start(bf16[2,8,16,384]{3,2,1,0:T(8,128)(2,1)} %own_hbm.1), channel_id=1, source_target_pairs={{0,2},{2,4},{4,6},{6,8},{8,10},{10,12},{12,14},{14,0},{1,3},{3,5},... | collective-permute-start | bytes 589832 | tf_op jit(solution)/shard_map/ppermute | solution.py:271
  3.6 0.0 collective-permute-done.own_far
  3.6 0.0 copy-start
  3.6 2.0 %pack.1 = (bf16[144,384]{1,0:T(8,128)(2,1)S(1)}, bf16[48,384]{1,0:T(8,128)(2,1)S(1)}, f32[16,128]{1,0:T(8,128)S(1)}, bf16[2,8,16,384]{3,2,1,0:T(8,128)(2,1)S(1)}...) custom-call(s32[1]{0:T(128)S(6)} %copy.10.counts, s32[16]{0:T(128)} %owners_hbm.1, ...), custom_call_target="tpu_custom_call" | custom-call | flops 10000000 | bytes 4194304 | tf_op jit(solution)/shard_map/pack/pallas_call | solution.py:273
  5.6 1.4 %collective-permute-start.2 = (bf16[48,384]{1,0:T(8,128)(2,1)S(1)}, bf16[48,384]{1,0:T(8,128)(2,1)S(1)}, u32[]{:S(2)}, u32[]{:S(2)}) collective-permute-start(bf16[48,384]{1,0:T(8,128)(2,1)S(1)} %get-tuple-element.20.marks), channel_id=1, source_target_pairs={{0,3},{1,2},{2,5},{3,4},{4,7},{5,6},{6,9},{7,8},{8,11},{9,10},{10,... | collective-permute-start | bytes 110600 | tf_op jit(solution)/shard_map/ppermute | solution.py:294
  7.0 1.6 %collective-permute-start.3 = (bf16[144,384]{1,0:T(8,128)(2,1)S(1)}, bf16[144,384]{1,0:T(8,128)(2,1)S(1)}, u32[]{:S(2)}, u32[]{:S(2)}) collective-permute-start(bf16[144,384]{1,0:T(8,128)(2,1)S(1)} %get-tuple-element.21), channel_id=1, source_target_pairs={{0,4},{2,6},{4,8},{6,10},{8,12},{10,14},{12,0},{14,2},{1,5},{3,7},... | collective-permute-start | bytes 331784 | tf_op jit(solution)/shard_map/ppermute | solution.py:293
  8.6 0.0 copy-done
  8.6 0.0 copy-start.1
  8.6 1.6 %local.1 = (f32[144,768]{1,0:T(8,128)S(1)}, f32[144,768]{1,0:T(8,128)S(1)}, bf16[768,256]{1,0:T(8,128)(2,1)S(1)}, bf16[2,384,768]{2,1,0:T(8,128)(2,1)S(1)}, bf16...) custom-call(bf16[2,8,16,384]{3,2,1,0:T(8,128)(2,1)S(1)} %get-tuple-element.23.own, ...), custom_call_target="tpu_custom_call" | custom-call | flops 600000000 | bytes 6291456 | tf_op jit(solution)/shard_map/local/pallas_call | solution.py:303
  10.3 1.7 %collective-permute-done.1.near = bf16[2,8,16,384]{3,2,1,0:T(8,128)(2,1)S(1)} collective-permute-done((bf16[2,8,16,384]{3,2,1,0:T(8,128)(2,1)}, bf16[2,8,16,384]{3,2,1,0:T(8,128)(2,1)S(1)}, u32[]{:S(2)}, u32[]{:S(2)}) %collective-permute-start.1) | collective-permute-done | bytes 196640 | tf_op jit(solution)/shard_map/ppermute | solution.py:271
  11.9 0.4 %collective-permute-done.2.edges = bf16[48,384]{1,0:T(8,128)(2,1)S(1)} collective-permute-done((bf16[48,384]{1,0:T(8,128)(2,1)S(1)}, bf16[48,384]{1,0:T(8,128)(2,1)S(1)}, u32[]{:S(2)}, u32[]{:S(2)}) %collective-permute-start.2) | collective-permute-done | bytes 36896 | tf_op jit(solution)/shard_map/ppermute | solution.py:294
  12.4 0.0 copy-done.1
  12.4 2.4 %near.1 = (bf16[4,16,6144]{2,1,0:T(8,128)(2,1)}, f32[144,768]{1,0:T(8,128)S(1)}) custom-call(bf16[48,384]{1,0:T(8,128)(2,1)S(1)} %get-tuple-element.20.marks, f32[16,128]{1,0:T(8,128)S(1)} %get-tuple-element.19.keep, bf16[2,8,16,384]{3,2,1,0:T(8,128)(2,1)S(1)} %collective-permute-done.1.near, bf16[48,384]{1,0:T(8,128)(2,1)S(1)} %collective-permute-done.2.edges, ...), custom_call_target="tpu_custom_call" | custom-call | flops 1000000000 | bytes 4194304 | tf_op jit(solution)/shard_map/near/pallas_call | solution.py:320
  14.8 0.0 collective-permute-done.3.far
  14.8 2.4 %far.1 = bf16[4,16,6144]{2,1,0:T(8,128)(2,1)} custom-call(f32[16,128]{1,0:T(8,128)S(1)} %get-tuple-element.19.keep, bf16[2,8,16,384]{3,2,1,0:T(8,128)(2,1)S(1)} %collective-permute-done.1.near, bf16[48,384]{1,0:T(8,128)(2,1)S(1)} %collective-permute-done.2.edges, bf16[144,384]{1,0:T(8,128)(2,1)S(1)} %collective-permute-done.3.far, ...), custom_call_target="tpu_custom_call", output_to_operand_aliasing={{}: (11, {})} | custom-call | flops 1000000000 | bytes 4194304 | tf_op jit(solution)/shard_map/far/pallas_call | solution.py:330
Async XLA Ops:
  0.0 3.6 %collective-permute-start = (bf16[2,8,16,384]{3,2,1,0:T(8,128)(2,1)}, bf16[2,8,16,384]{3,2,1,0:T(8,128)(2,1)S(1)}, u32[]{:S(2)}, u32[]{:S(2)}) collective-permute-start(bf16[2,8,16,384]{3,2,1,0:T(8,128)(2,1)} %own_hbm.1), channel_id=1, source_target_pairs={{0,1},{1,0},{2,3},{3,2},{4,5},{5,4},{6,7},{7,6},{8,9},{9,8},{10,11... | collective-permute-start | bytes 589832 | tf_op jit(solution)/shard_map/ppermute | solution.py:272
  0.5 11.5 %collective-permute-start.1 = (bf16[2,8,16,384]{3,2,1,0:T(8,128)(2,1)}, bf16[2,8,16,384]{3,2,1,0:T(8,128)(2,1)S(1)}, u32[]{:S(2)}, u32[]{:S(2)}) collective-permute-start(bf16[2,8,16,384]{3,2,1,0:T(8,128)(2,1)} %own_hbm.1), channel_id=1, source_target_pairs={{0,2},{2,4},{4,6},{6,8},{8,10},{10,12},{12,14},{14,0},{1,3},{3,5},... | collective-permute-start | bytes 589832 | tf_op jit(solution)/shard_map/ppermute | solution.py:271
  3.6 5.0 %copy-start = (f32[768]{0:T(1024)S(1)}, f32[768]{0:T(1024)}, u32[]{:S(2)}) copy-start(f32[768]{0:T(1024)} %b_time.1) | copy-start | bytes 9220
  5.6 6.7 %collective-permute-start.2 = (bf16[48,384]{1,0:T(8,128)(2,1)S(1)}, bf16[48,384]{1,0:T(8,128)(2,1)S(1)}, u32[]{:S(2)}, u32[]{:S(2)}) collective-permute-start(bf16[48,384]{1,0:T(8,128)(2,1)S(1)} %get-tuple-element.20.marks), channel_id=1, source_target_pairs={{0,3},{1,2},{2,5},{3,4},{4,7},{5,6},{6,9},{7,8},{8,11},{9,10},{10,... | collective-permute-start | bytes 110600 | tf_op jit(solution)/shard_map/ppermute | solution.py:294
  7.0 7.7 %collective-permute-start.3 = (bf16[144,384]{1,0:T(8,128)(2,1)S(1)}, bf16[144,384]{1,0:T(8,128)(2,1)S(1)}, u32[]{:S(2)}, u32[]{:S(2)}) collective-permute-start(bf16[144,384]{1,0:T(8,128)(2,1)S(1)} %get-tuple-element.21), channel_id=1, source_target_pairs={{0,4},{2,6},{4,8},{6,10},{8,12},{10,14},{12,0},{14,2},{1,5},{3,7},... | collective-permute-start | bytes 331784 | tf_op jit(solution)/shard_map/ppermute | solution.py:293
  8.6 3.7 %copy-start.1 = (f32[192]{0:T(256)S(1)}, f32[192]{0:T(256)}, u32[]{:S(2)}) copy-start(f32[192]{0:T(256)} %b_up.3) | copy-start | bytes 2308

commit v4 on v2

v4 whole, which is shorter than its diff:
```python
import jax
import jax.numpy as jnp
from jax import lax
from jax.experimental import pallas as pl
from jax.experimental.pallas import tpu as pltpu
from jax.sharding import PartitionSpec as P

OV = 4
F32 = jnp.float32
BF16 = jnp.bfloat16
VMEM = pl.BlockSpec(memory_space=pltpu.VMEM)
SMEM = pl.BlockSpec(memory_space=pltpu.SMEM)
HBM = pl.BlockSpec(memory_space=pltpu.HBM)
LEAVES = 4
ABSENT = 16384.0
PARAMS = pltpu.CompilerParams(vmem_limit_bytes=24 << 20)


def dot(a, b):
    return jnp.dot(a, b, preferred_element_type=F32)


def dot_t(a, b):
    return lax.dot_general(a, b, (((1,), (1,)), ((), ())), preferred_element_type=F32)


def cost(flops, moved):
    return pl.CostEstimate(flops=flops, bytes_accessed=moved, transcendentals=0)


def prepare_weights(w_up, wc, wl, wr):
    outc, chans = w_up.shape[2], w_up.shape[3]
    pad = wl.shape[1] - outc
    for pr, block, rows in ((1, 1, (2,)), (0, 1, (1, 2)), (1, 0, (0, 1)), (0, 0, (0,))):
        taps = []
        for col in range(3):
            tap = w_up[rows[0], col].astype(F32)
            for row in rows[1:]:
                tap = tap + w_up[row, col].astype(F32)
            taps.append(tap)
        span = pl.ds(block * chans, chans)
        wc[pr, pl.ds(0, outc), span] = (taps[1] + taps[2]).astype(BF16)
        wc[pr, pl.ds(outc, outc), span] = (taps[0] + taps[1]).astype(BF16)
        wl[pr, pl.ds(0, outc), span] = taps[0].astype(BF16)
        wl[pr, pl.ds(outc, pad), span] = jnp.zeros((pad, chans), BF16)
        wr[pr, pl.ds(0, pad), span] = jnp.zeros((pad, chans), BF16)
        wr[pr, pl.ds(pad, outc), span] = taps[2].astype(BF16)


def turner(rows, cols):
    i = lax.broadcasted_iota(jnp.int32, (rows * cols, rows * cols), 0)
    k = lax.broadcasted_iota(jnp.int32, (rows * cols, rows * cols), 1)
    return jnp.where(k == (i % rows) * cols + i // rows, 1.0, 0.0).astype(BF16)


def picker(rows, cols, col):
    i = lax.broadcasted_iota(jnp.int32, (2 * rows, rows * cols), 0)
    k = lax.broadcasted_iota(jnp.int32, (2 * rows, rows * cols), 1)
    return jnp.where((i < rows) & (k == i * cols + col), 1.0, 0.0).astype(BF16)


def fill_x(t, mine, x, rows, cols):
    chans = t.shape[1] // 2
    t = t.astype(BF16).astype(F32)
    row = lax.broadcasted_iota(jnp.int32, (rows, 2 * chans), 0)
    for col in range(cols + 1):
        one = t[col * rows : (col + 1) * rows]
        up = jnp.where(row == 0, 0.0, pltpu.roll(one, 1, 0))
        down = jnp.where(row == rows - 1, 0.0, pltpu.roll(one, rows - 1, 0))
        for v, shifted in enumerate((up, one, down)):
            lanes = pl.ds(v * chans, chans)
            column = jnp.concatenate([shifted[:, :chans], shifted[:, chans:]], 0)
            if col < cols:
                x[pl.ds((col + 1) * 2 * rows, 2 * rows), lanes] = column.astype(BF16)
            else:
                x[pl.ds(0, 2 * rows), lanes] = jnp.where(mine == 1, column, 0.0).astype(BF16)
                x[pl.ds((cols + 1) * 2 * rows, 2 * rows), lanes] = jnp.where(mine == 0, column, 0.0).astype(BF16)


def convolve(x, wc, wl, wr, b_up, keep, mine, wide, done, rows, cols, copies):
    chans2 = wc.shape[2]
    chans = chans2 // 2
    height = 2 * rows * cols
    lanes = wc.shape[1]
    part = wl.shape[1]
    col_of = lax.broadcasted_iota(jnp.int32, (height, 1), 0) // (2 * rows)
    strip_from = jnp.where(mine == 0, cols - OV, 0)
    soft = 1.0 - 0.5 / (2 * OV)
    scale_l = jnp.where(col_of == strip_from, soft, 1.0)
    scale_r = jnp.where(col_of == strip_from + OV - 1, soft, 1.0)
    bias = b_up[...].reshape(1, -1)
    bias = jnp.concatenate([bias, bias], -1)
    for pr in range(2):
        span = pl.ds(pr * chans, chans2)
        mid = dot_t(x[pl.ds(2 * rows, height), span], wc[pr])
        left = dot_t(x[pl.ds(0, height), span], wl[pr]) * scale_l
        right = dot_t(x[pl.ds(4 * rows, height), span], wr[pr]) * scale_r
        low = mid[:, : lanes - part] + left[:, : lanes - part]
        centre = mid[:, lanes - part : part] + left[:, lanes - part :] + right[:, : 2 * part - lanes]
        high = mid[:, part:] + right[:, 2 * part - lanes :]
        y = jnp.concatenate([low, centre, high], -1) + bias
        for col in range(cols):
            for h in range(2):
                top = col * 2 * rows + h * rows
                for j in range(lanes // 128):
                    wide[h, col * lanes // 128 + j, pl.ds(pr, rows, stride=2), :] = y[
                        top : top + rows, j * 128 : (j + 1) * 128
                    ]
    keep = keep[...] > 0.5
    for col in range(cols):
        shared = col < OV or col >= cols - OV
        outside = (col < strip_from) | (col >= strip_from + OV)
        for h in range(2):
            for lane in range(col * lanes, (col + 1) * lanes, 128):
                block = wide[h, lane // 128]
                if shared:
                    block = jnp.where(keep | outside, block, 0.0)
                done[h, :, pl.ds(lane, 128)] = block.astype(BF16)
        if copies and (col + 1) % (cols // LEAVES) == 0:
            copies[col // (cols // LEAVES)].start()


def leave(done, out, sems):
    width = done.shape[2] // LEAVES
    spans = [pl.ds(k * width, width) for k in range(LEAVES)]
    return [
        pltpu.make_async_copy(done.at[:, :, span], out.at[:, :, span], sems.at[k])
        for k, span in enumerate(spans)
    ]


def load_kernel(owners_hbm, own_hbm, b_time_hbm, b_up_hbm, keep, own, b_time, b_up, owners, sems):
    pairs = [(own_hbm, own), (owners_hbm, owners), (b_time_hbm, b_time), (b_up_hbm, b_up)]
    loads = [pltpu.make_async_copy(source, target, sems.at[k]) for k, (source, target) in enumerate(pairs)]
    for load in loads:
        load.start()
    mine = lax.axis_index("tile")
    for load in loads:
        load.wait()
    out_row = lax.broadcasted_iota(jnp.int32, keep.shape, 0)
    owner = jnp.zeros(keep.shape, jnp.int32)
    for r in range(keep.shape[0]):
        owner = jnp.where(out_row == r, owners[r], owner)
    keep[...] = jnp.where(owner == mine, 1.0, 0.0)


def pack_kernel(counts, own, own_far, latest, before):
    slots, rows, cols, chans = own.shape
    pixels = rows * cols
    mine = lax.axis_index("tile")
    two = counts[0] >= 2
    turn = turner(rows, cols)
    pick = picker(rows, cols, jnp.where(mine == 0, OV, cols - OV - 1))
    first, second = own[0].reshape(pixels, chans), own[1].reshape(pixels, chans)
    first_far, second_far = own_far[0].reshape(pixels, chans), own_far[1].reshape(pixels, chans)
    latest[pl.ds(0, pixels), :] = dot(turn, jnp.where(two, second, first)).astype(BF16)
    latest[pl.ds(pixels, 2 * rows), :] = dot(pick, jnp.where(two, second_far, first_far)).astype(BF16)
    before[pl.ds(0, pixels), :] = jnp.where(two, dot(turn, first), ABSENT).astype(BF16)
    before[pl.ds(pixels, 2 * rows), :] = jnp.where(two, dot(pick, first_far), ABSENT).astype(BF16)


def local_kernel(latest, before, w_time, b_time, w_up, t0, t1, wc, wl, wr, lhs):
    two = is_there(before)
    lhs[...] = jnp.where(two, before[...], latest[...])
    prepare_weights(w_up, wc, wl, wr)
    bias = b_time[...].reshape(1, -1)
    t0[...] = bias + dot(lhs[...], w_time[2])

    @pl.when(two)
    def _():
        t1[...] = bias + dot(latest[...], w_time[2]) + dot(lhs[...], w_time[1])


def is_there(frame):
    return jnp.max(frame[pl.ds(0, 16), pl.ds(0, 128)].astype(F32)) < 0.5 * ABSENT


def near_kernel(before, keep, newer, w_time, b_up, t0, t1, wc, wl, wr, done, t0_new, lhs, x, wide):
    rows = keep.shape[0] // 2
    cols = (newer.shape[0] - 2 * rows) // rows
    mine = lax.axis_index("tile")
    lhs[...] = jnp.where(lax.axis_index("tm") == 0, jnp.zeros_like(newer), newer[...])
    valid = is_there(before)

    @pl.when(valid)
    def _():
        t = t1[...] + dot(lhs[...], w_time[0])
        fill_x(t, mine, x, rows, cols)
        convolve(x, wc, wl, wr, b_up, keep, mine, wide, done, rows, cols, [])

    @pl.when(jnp.logical_not(valid))
    def _():
        done[...] = jnp.zeros_like(done)

    t0_new[...] = t0[...] + dot(lhs[...], w_time[1])


def far_kernel(
    keep, near_before, far, w_time, b_up, t0, wc, wl, wr, second, out, lhs, x, wide, done, sems
):
    early = pltpu.make_async_copy(second, out.at[pl.ds(2, 2)], sems.at[LEAVES])
    early.start()
    rows = keep.shape[0] // 2
    cols = (far.shape[0] - 2 * rows) // rows
    mine = lax.axis_index("tile")
    place_tm = lax.axis_index("tm")
    two = is_there(near_before)
    older = jnp.where(two, near_before[...], far[...])
    none = (place_tm == 0) | ((place_tm == 1) & jnp.logical_not(two))
    lhs[...] = jnp.where(none, jnp.zeros_like(older), older)
    t = t0[...] + dot(lhs[...], w_time[0])
    fill_x(t, mine, x, rows, cols)
    copies = leave(done, out.at[pl.ds(0, 2)], sems)
    convolve(x, wc, wl, wr, b_up, keep, mine, wide, done, rows, cols, copies)
    for copy in copies + [early]:
        copy.wait()


def per_device(latents, frame_counts, owners, w_time, b_time, w_up, b_up):
    slots, rows, cols, chans = latents.shape
    outc = w_up.shape[3]
    ring = lax.axis_size("tm")
    pixels, extra = rows * cols, 2 * rows
    lanes = 2 * cols * outc
    shape = jax.ShapeDtypeStruct

    def step(k):
        return [(i, (i + k) % ring) for i in range(ring)]

    def stay(v):
        return pltpu.with_memory_space_constraint(v, pltpu.HBM)

    w_up = w_up.transpose(0, 1, 3, 2)
    own_far = lax.ppermute(latents, "tile", [(0, 1), (1, 0)])
    keep, own, b_time, b_up = pl.pallas_call(
        load_kernel,
        out_shape=(
            shape((extra, 128), F32),
            shape(latents.shape, BF16),
            shape(b_time.shape, F32),
            shape(b_up.shape, F32),
        ),
        in_specs=[HBM] * 4,
        out_specs=(VMEM,) * 4,
        scratch_shapes=[pltpu.SMEM(owners.shape, jnp.int32), pltpu.SemaphoreType.DMA((4,))],
        compiler_params=PARAMS,
        cost_estimate=cost(10**6, 1 << 10),
        name="load",
    )(stay(owners), stay(latents), stay(b_time), stay(b_up))
    frame = shape((pixels + extra, chans), BF16)
    latest, before = pl.pallas_call(
        pack_kernel,
        out_shape=(frame, frame),
        in_specs=[SMEM, VMEM, VMEM],
        out_specs=(VMEM,) * 2,
        compiler_params=PARAMS,
        cost_estimate=cost(3 * 10**9, 1 << 10),
        name="pack",
    )(frame_counts, own, own_far)
    newer = lax.ppermute(latest, "tm", step(1))
    far = lax.ppermute(latest, "tm", [(i, i + 2) for i in range(ring - 2)])
    near_before = lax.ppermute(before, "tm", step(1))
    partial = shape((pixels + extra, 2 * chans), F32)
    scratch = [
        pltpu.VMEM(frame.shape, BF16),
        pltpu.VMEM(((cols + 2) * extra, 3 * chans), BF16),
        pltpu.VMEM((2, lanes // 128, extra, 128), F32),
        pltpu.VMEM((2, extra, lanes), BF16),
        pltpu.SemaphoreType.DMA((LEAVES + 1,)),
    ]
    t0, t1, wc, wl, wr = pl.pallas_call(
        local_kernel,
        out_shape=(
            partial,
            partial,
            shape((2, 2 * outc, 2 * chans), BF16),
            shape((2, 256, 2 * chans), BF16),
            shape((2, 256, 2 * chans), BF16),
        ),
        in_specs=[VMEM] * 5,
        out_specs=(VMEM,) * 5,
        scratch_shapes=[pltpu.VMEM(frame.shape, BF16)],
        compiler_params=PARAMS,
        cost_estimate=cost(10**6, 1 << 10),
        name="local",
    )(latest, before, w_time, b_time, w_up)
    second, t0 = pl.pallas_call(
        near_kernel,
        out_shape=(shape((2, 2 * rows, lanes), BF16), partial),
        in_specs=[VMEM] * 10,
        out_specs=(VMEM, VMEM),
        scratch_shapes=scratch[:3],
        compiler_params=PARAMS,
        cost_estimate=cost(10**9, 4 << 20),
        name="near",
    )(before, keep, newer, w_time, b_up, t0, t1, wc, wl, wr)
    return pl.pallas_call(
        far_kernel,
        out_shape=shape((2 * slots, 2 * rows, lanes), BF16),
        in_specs=[VMEM] * 10,
        out_specs=HBM,
        scratch_shapes=scratch,
        compiler_params=PARAMS,
        cost_estimate=cost(10**9, 4 << 20),
        name="far",
    )(keep, near_before, far, w_time, b_up, t0, wc, wl, wr, second)


def solution(mesh):
    placed = (
        P(("videos", "tm"), None, "tile", None),
        P(("videos", "tm")),
        P("videos"),
        P(),
        P(),
        P(),
        P(),
    )
    return jax.shard_map(
        per_device,
        mesh=mesh,
        in_specs=placed,
        out_specs=P(("videos", "tm"), None, "tile"),
        check_vma=False,
    )
```

time: 19.1 us -> 16.3 us (0.85)
  local copies, waits for them, and re-layouts: 4.43 us -> 0.01 us
  starting transfers between devices: 5.93 us -> 8.02 us
  Pallas kernels: 7.8 us -> 6.44 us
  waiting for transfers between devices: 0.01 us -> 0.96 us
    unnamed x12 -> x4, local copies, waits for them, and re-layouts: 3.74 us -> 0.01 us
    ppermute x4, starting transfers between devices: 5.93 us -> 8.02 us  [the longest x1 3.47 us: per_device(): far = lax.ppermute(latest, 'tm', [(i, i + 2) for i in range(ring - 2)])]
    pallas_call x4 -> x5, Pallas kernels: 7.8 us -> 6.44 us  [the longest x1 2.12 us: per_device(): pl.pallas_call(far_kernel, out_shape=shape((2 * slots, 2 * rows, lanes),...]
    ppermute x4, waiting for transfers between devices: 0.01 us -> 0.96 us  [the longest x1 0.51 us: per_device(): newer = lax.ppermute(latest, 'tm', step(1))]
    reshape x1 -> x0, local copies, waits for them, and re-layouts: 0.69 us -> none  [per_device(): b_time = b_time.reshape(1, -1)]
  transfers between devices with their start and end apart: 4 -> 4, of which waited for: 0 -> 2; matrix products, arithmetic and copies ran while one was open for 4% -> 0% of each run, Pallas kernels for 26% -> 25%
where the time goes in v4:
time: 16.3 us; the launch traced here: 16.2 us
  starting transfers between devices  8.02 us (49%)
  Pallas kernels  6.44 us (40%)
  waiting for transfers between devices  0.96 us (6%)
  between operations  0.73 us (4%)
    ppermute x1, starting transfers between devices, per_device(): far = lax.ppermute(latest, 'tm', [(i, i + 2) for i in range(ring - 2)])  3.47 us
    ppermute x1, starting transfers between devices, per_device(): newer = lax.ppermute(latest, 'tm', step(1))  2.54 us
    pallas_call x1, Pallas kernels, per_device(): pl.pallas_call(far_kernel, out_shape=shape((2 * slots, 2 * rows, lanes),...  2.12 us
    pallas_call x1, Pallas kernels, per_device(): pl.pallas_call(near_kernel, out_shape=(shape((2, 2 * rows, lanes), BF16),...  1.73 us
    ppermute x1, starting transfers between devices, per_device(): near_before = lax.ppermute(before, 'tm', step(1))  1.55 us
    pallas_call x1, Pallas kernels, per_device(): pl.pallas_call(local_kernel, out_shape=(partial, partial, shape((2, 2 * o...  1.38 us
    pallas_call x1, Pallas kernels, per_device(): pl.pallas_call(load_kernel, out_shape=(shape((extra, 128), F32), shape(la...  0.99 us
    ppermute x1, waiting for transfers between devices, per_device(): newer = lax.ppermute(latest, 'tm', step(1))  0.51 us
  transfers between devices with their start and end apart: 4, of which 2 were waited for; matrix products, arithmetic and copies ran while one was open for 0% of the time, Pallas kernels for 25%

profile of v4, /device:TPU:0, one launch (start us, length us, event | category | flops | bytes accessed | tf_op | source)
XLA Modules:
  0.0 16.2 jit_solution(10937085538081059636)
XLA Ops:
  0.0 0.5 %collective-permute-start = (bf16[2,8,16,384]{3,2,1,0:T(8,128)(2,1)}, bf16[2,8,16,384]{3,2,1,0:T(8,128)(2,1)S(1)}, u32[]{:S(2)}, u32[]{:S(2)}) collective-permute-start(bf16[2,8,16,384]{3,2,1,0:T(8,128)(2,1)} %own_hbm.1), channel_id=1, source_target_pairs={{0,1},{1,0},{2,3},{3,2},{4,5},{5,4},{6,7},{7,6},{8,9},{9,8},{10,11... | collective-permute-start | bytes 589832 | tf_op jit(solution)/shard_map/ppermute | solution.py:234
  1.1 1.0 %load.1 = (f32[16,128]{1,0:T(8,128)S(1)}, bf16[2,8,16,384]{3,2,1,0:T(8,128)(2,1)S(1)}, f32[768]{0:T(1024)S(1)}, f32[192]{0:T(256)S(1)}) custom-call(s32[16]{0:T(128)} %owners_hbm.1, bf16[2,8,16,384]{3,2,1,0:T(8,128)(2,1)} %own_hbm.1, f32[768]{0:T(1024)} %b_time_hbm.1, f32[192]{0:T(256)} %b_up_hbm.1), custom_call_target="tpu_custom_call" | custom-call | flops 1000000 | bytes 1024 | tf_op jit(solution)/shard_map/load/pallas_call | solution.py:235
  2.1 0.0 collective-permute-done.own_far
  2.1 0.0 copy-start
  2.1 0.0 copy-start.1
  2.1 0.2 %pack.1 = (bf16[144,384]{1,0:T(8,128)(2,1)S(1)}, bf16[144,384]{1,0:T(8,128)(2,1)S(1)}) custom-call(s32[1]{0:T(128)S(6)} %copy.8.counts, bf16[2,8,16,384]{3,2,1,0:T(8,128)(2,1)S(1)} %get-tuple-element.19.own, bf16[2,8,16,384]{3,2,1,0:T(8,128)(2,1)S(1)} %collective-permute-done.own_far), custom_call_target="tpu_custom_call" | custom-call | flops 3000000000 | bytes 1024 | tf_op jit(solution)/shard_map/pack/pallas_call | solution.py:251
  2.4 2.5 %collective-permute-start.3 = (bf16[144,384]{1,0:T(8,128)(2,1)S(1)}, bf16[144,384]{1,0:T(8,128)(2,1)S(1)}, u32[]{:S(2)}, u32[]{:S(2)}) collective-permute-start(bf16[144,384]{1,0:T(8,128)(2,1)S(1)} %get-tuple-element.21.latest), channel_id=1, source_target_pairs={{0,2},{2,4},{4,6},{6,8},{8,10},{10,12},{12,14},{14,0},{1,3},{3,5},... | collective-permute-start | bytes 331784 | tf_op jit(solution)/shard_map/ppermute | solution.py:260
  4.9 1.5 %collective-permute-start.1 = (bf16[144,384]{1,0:T(8,128)(2,1)S(1)}, bf16[144,384]{1,0:T(8,128)(2,1)S(1)}, u32[]{:S(2)}, u32[]{:S(2)}) collective-permute-start(bf16[144,384]{1,0:T(8,128)(2,1)S(1)} %get-tuple-element.20.before), channel_id=1, source_target_pairs={{0,2},{2,4},{4,6},{6,8},{8,10},{10,12},{12,14},{14,0},{1,3},{3,5},... | collective-permute-start | bytes 331784 | tf_op jit(solution)/shard_map/ppermute | solution.py:262
  6.5 3.5 %collective-permute-start.2 = (bf16[144,384]{1,0:T(8,128)(2,1)S(1)}, bf16[144,384]{1,0:T(8,128)(2,1)S(1)}, u32[]{:S(2)}, u32[]{:S(2)}) collective-permute-start(bf16[144,384]{1,0:T(8,128)(2,1)S(1)} %get-tuple-element.21.latest), channel_id=1, source_target_pairs={{0,4},{2,6},{4,8},{6,10},{8,12},{10,14},{1,5},{3,7},{5,9},{7,11},{... | collective-permute-start | bytes 331784 | tf_op jit(solution)/shard_map/ppermute | solution.py:261
  9.9 0.0 copy-done
  9.9 0.0 copy-done.1
  10.0 1.4 %local.1 = (f32[144,768]{1,0:T(8,128)S(1)}, f32[144,768]{1,0:T(8,128)S(1)}, bf16[2,384,768]{2,1,0:T(8,128)(2,1)S(1)}, bf16[2,256,768]{2,1,0:T(8,128)(2,1)S(1)}, bf16[2,256,768]{2,1,0:T(8,128)(2,1)S(1)}) custom-call(bf16[144,384]{1,0:T(8,128)(2,1)S(1)} %get-tuple-element.21.latest, bf16[144,384]{1,0:T(8,128)(2,1)S(1)} %get-tuple-element.20.before, ...), custom_call_target="tpu_custom_call" | custom-call | flops 1000000 | bytes 1024 | tf_op jit(solution)/shard_map/local/pallas_call | solution.py:271
  11.3 0.5 %collective-permute-done.3.newer = bf16[144,384]{1,0:T(8,128)(2,1)S(1)} collective-permute-done((bf16[144,384]{1,0:T(8,128)(2,1)S(1)}, bf16[144,384]{1,0:T(8,128)(2,1)S(1)}, u32[]{:S(2)}, u32[]{:S(2)}) %collective-permute-start.3) | collective-permute-done | bytes 110624 | tf_op jit(solution)/shard_map/ppermute | solution.py:260
  11.9 1.7 %near.1 = (bf16[2,16,6144]{2,1,0:T(8,128)(2,1)S(1)}, f32[144,768]{1,0:T(8,128)S(1)}) custom-call(bf16[144,384]{1,0:T(8,128)(2,1)S(1)} %get-tuple-element.20.before, f32[16,128]{1,0:T(8,128)S(1)} %get-tuple-element.18.keep, bf16[144,384]{1,0:T(8,128)(2,1)S(1)} %collective-permute-done.3.newer, bf16[3,384,768]{2,1,0:T(8,128)(2,1)S(1)} %copy-done, ...), custom_call_target="tpu_custom_call" | custom-call | flops 1000000000 | bytes 4194304 | tf_op jit(solution)/shard_map/near/pallas_call | solution.py:287
  13.6 0.4 %collective-permute-done.1.near_before = bf16[144,384]{1,0:T(8,128)(2,1)S(1)} collective-permute-done((bf16[144,384]{1,0:T(8,128)(2,1)S(1)}, bf16[144,384]{1,0:T(8,128)(2,1)S(1)}, u32[]{:S(2)}, u32[]{:S(2)}) %collective-permute-start.1) | collective-permute-done | bytes 110624 | tf_op jit(solution)/shard_map/ppermute | solution.py:262
  14.0 0.0 collective-permute-done.2.far
  14.0 2.1 %far.1 = bf16[4,16,6144]{2,1,0:T(8,128)(2,1)} custom-call(f32[16,128]{1,0:T(8,128)S(1)} %get-tuple-element.18.keep, bf16[144,384]{1,0:T(8,128)(2,1)S(1)} %collective-permute-done.1.near_before, bf16[144,384]{1,0:T(8,128)(2,1)S(1)} %collective-permute-done.2.far, bf16[3,384,768]{2,1,0:T(8,128)(2,1)S(1)} %copy-done, f32[192]{0:T(256)S(1)} %get-tuple-element.22.b_up, ...), custom_call_target="tpu_custom_call" | custom-call | flops 1000000000 | bytes 4194304 | tf_op jit(solution)/shard_map/far/pallas_call | solution.py:297
Async XLA Ops:
  0.0 2.1 %collective-permute-start = (bf16[2,8,16,384]{3,2,1,0:T(8,128)(2,1)}, bf16[2,8,16,384]{3,2,1,0:T(8,128)(2,1)S(1)}, u32[]{:S(2)}, u32[]{:S(2)}) collective-permute-start(bf16[2,8,16,384]{3,2,1,0:T(8,128)(2,1)} %own_hbm.1), channel_id=1, source_target_pairs={{0,1},{1,0},{2,3},{3,2},{4,5},{5,4},{6,7},{7,6},{8,9},{9,8},{10,11... | collective-permute-start | bytes 589832 | tf_op jit(solution)/shard_map/ppermute | solution.py:234
  2.1 7.8 %copy-start = (bf16[3,384,768]{2,1,0:T(8,128)(2,1)S(1)}, bf16[3,384,768]{2,1,0:T(8,128)(2,1)}, u32[]{:S(2)}) copy-start(bf16[3,384,768]{2,1,0:T(8,128)(2,1)} %w_time.5) | copy-start | bytes 5308420
  2.1 7.8 %copy-start.1 = (bf16[3,3,384,192]{2,3,1,0:T(8,128)(2,1)S(1)}, bf16[3,3,384,192]{2,3,1,0:T(8,128)(2,1)}, u32[]{:S(2)}) copy-start(bf16[3,3,384,192]{2,3,1,0:T(8,128)(2,1)} %param.12) | copy-start | bytes 3981316
  2.4 9.5 %collective-permute-start.3 = (bf16[144,384]{1,0:T(8,128)(2,1)S(1)}, bf16[144,384]{1,0:T(8,128)(2,1)S(1)}, u32[]{:S(2)}, u32[]{:S(2)}) collective-permute-start(bf16[144,384]{1,0:T(8,128)(2,1)S(1)} %get-tuple-element.21.latest), channel_id=1, source_target_pairs={{0,2},{2,4},{4,6},{6,8},{8,10},{10,12},{12,14},{14,0},{1,3},{3,5},... | collective-permute-start | bytes 331784 | tf_op jit(solution)/shard_map/ppermute | solution.py:260
  4.9 9.1 %collective-permute-start.1 = (bf16[144,384]{1,0:T(8,128)(2,1)S(1)}, bf16[144,384]{1,0:T(8,128)(2,1)S(1)}, u32[]{:S(2)}, u32[]{:S(2)}) collective-permute-start(bf16[144,384]{1,0:T(8,128)(2,1)S(1)} %get-tuple-element.20.before), channel_id=1, source_target_pairs={{0,2},{2,4},{4,6},{6,8},{8,10},{10,12},{12,14},{14,0},{1,3},{3,5},... | collective-permute-start | bytes 331784 | tf_op jit(solution)/shard_map/ppermute | solution.py:262
  6.5 7.6 %collective-permute-start.2 = (bf16[144,384]{1,0:T(8,128)(2,1)S(1)}, bf16[144,384]{1,0:T(8,128)(2,1)S(1)}, u32[]{:S(2)}, u32[]{:S(2)}) collective-permute-start(bf16[144,384]{1,0:T(8,128)(2,1)S(1)} %get-tuple-element.21.latest), channel_id=1, source_target_pairs={{0,4},{2,6},{4,8},{6,10},{8,12},{10,14},{1,5},{3,7},{5,9},{7,11},{... | collective-permute-start | bytes 331784 | tf_op jit(solution)/shard_map/ppermute | solution.py:261

commit v5 on v4

--- a/solution.py
+++ b/solution.py
@@ -28,9 +28,8 @@
     return pl.CostEstimate(flops=flops, bytes_accessed=moved, transcendentals=0)
 
 
-def prepare_weights(w_up, wc, wl, wr):
+def prepare_weights(w_up, wp):
     outc, chans = w_up.shape[2], w_up.shape[3]
-    pad = wl.shape[1] - outc
     for pr, block, rows in ((1, 1, (2,)), (0, 1, (1, 2)), (1, 0, (0, 1)), (0, 0, (0,))):
         taps = []
         for col in range(3):
@@ -38,13 +37,8 @@
             for row in rows[1:]:
                 tap = tap + w_up[row, col].astype(F32)
             taps.append(tap)
-        span = pl.ds(block * chans, chans)
-        wc[pr, pl.ds(0, outc), span] = (taps[1] + taps[2]).astype(BF16)
-        wc[pr, pl.ds(outc, outc), span] = (taps[0] + taps[1]).astype(BF16)
-        wl[pr, pl.ds(0, outc), span] = taps[0].astype(BF16)
-        wl[pr, pl.ds(outc, pad), span] = jnp.zeros((pad, chans), BF16)
-        wr[pr, pl.ds(0, pad), span] = jnp.zeros((pad, chans), BF16)
-        wr[pr, pl.ds(pad, outc), span] = taps[2].astype(BF16)
+        for k, tap in enumerate((taps[1] + taps[2], taps[0] + taps[1], taps[0], taps[2])):
+            wp[pr, pl.ds(k * outc, outc), pl.ds(block * chans, chans)] = tap.astype(BF16)
 
 
 def turner(rows, cols):
@@ -77,35 +71,41 @@
                 x[pl.ds((cols + 1) * 2 * rows, 2 * rows), lanes] = jnp.where(mine == 0, column, 0.0).astype(BF16)
 
 
-def convolve(x, wc, wl, wr, b_up, keep, mine, wide, done, rows, cols, copies):
-    chans2 = wc.shape[2]
+def convolve(x, wp, b_up, keep, mine, wide, done, rows, cols, copies):
+    chans2 = wp.shape[2]
     chans = chans2 // 2
-    height = 2 * rows * cols
-    lanes = wc.shape[1]
-    part = wl.shape[1]
-    col_of = lax.broadcasted_iota(jnp.int32, (height, 1), 0) // (2 * rows)
+    column = 2 * rows
+    outc = wp.shape[1] // 4
+    lanes = 2 * outc
     strip_from = jnp.where(mine == 0, cols - OV, 0)
     soft = 1.0 - 0.5 / (2 * OV)
-    scale_l = jnp.where(col_of == strip_from, soft, 1.0)
-    scale_r = jnp.where(col_of == strip_from + OV - 1, soft, 1.0)
     bias = b_up[...].reshape(1, -1)
     bias = jnp.concatenate([bias, bias], -1)
+    before_half = lax.broadcasted_iota(jnp.int32, (column, 128), 1) < outc % 128
     for pr in range(2):
-        span = pl.ds(pr * chans, chans2)
-        mid = dot_t(x[pl.ds(2 * rows, height), span], wc[pr])
-        left = dot_t(x[pl.ds(0, height), span], wl[pr]) * scale_l
-        right = dot_t(x[pl.ds(4 * rows, height), span], wr[pr]) * scale_r
-        low = mid[:, : lanes - part] + left[:, : lanes - part]
-        centre = mid[:, lanes - part : part] + left[:, lanes - part :] + right[:, : 2 * part - lanes]
-        high = mid[:, part:] + right[:, 2 * part - lanes :]
-        y = jnp.concatenate([low, centre, high], -1) + bias
+        z = dot_t(x[:, pl.ds(pr * chans, chans2)], wp[pr])
         for col in range(cols):
+            scale_l = scale_r = 1.0
+            if col in (0, cols - OV):
+                scale_l = jnp.where(strip_from == col, soft, 1.0)
+            if col in (OV - 1, cols - 1):
+                scale_r = jnp.where(strip_from + OV - 1 == col, soft, 1.0)
+            here = z[(col + 1) * column : (col + 2) * column, :lanes] + bias
+            prev = z[col * column : (col + 1) * column, lanes:] * scale_l
+            after = z[(col + 2) * column : (col + 3) * column, lanes:] * scale_r
+            tiles = []
+            for j in range(lanes // 128):
+                span = slice(j * 128, (j + 1) * 128)
+                if (j + 1) * 128 <= outc:
+                    add = prev[:, span]
+                elif j * 128 >= outc:
+                    add = after[:, span]
+                else:
+                    add = jnp.where(before_half, prev[:, span], after[:, span])
+                tiles.append(here[:, span] + add)
             for h in range(2):
-                top = col * 2 * rows + h * rows
-                for j in range(lanes // 128):
-                    wide[h, col * lanes // 128 + j, pl.ds(pr, rows, stride=2), :] = y[
-                        top : top + rows, j * 128 : (j + 1) * 128
-                    ]
+                for j, tile in enumerate(tiles):
+                    wide[h, col * lanes // 128 + j, pl.ds(pr, rows, stride=2), :] = tile[h * rows : (h + 1) * rows]
     keep = keep[...] > 0.5
     for col in range(cols):
         shared = col < OV or col >= cols - OV
@@ -159,10 +159,10 @@
     before[pl.ds(pixels, 2 * rows), :] = jnp.where(two, dot(pick, first_far), ABSENT).astype(BF16)
 
 
-def local_kernel(latest, before, w_time, b_time, w_up, t0, t1, wc, wl, wr, lhs):
+def local_kernel(latest, before, w_time, b_time, w_up, t0, t1, wp, lhs):
     two = is_there(before)
     lhs[...] = jnp.where(two, before[...], latest[...])
-    prepare_weights(w_up, wc, wl, wr)
+    prepare_weights(w_up, wp)
     bias = b_time[...].reshape(1, -1)
     t0[...] = bias + dot(lhs[...], w_time[2])
 
@@ -175,7 +175,7 @@
     return jnp.max(frame[pl.ds(0, 16), pl.ds(0, 128)].astype(F32)) < 0.5 * ABSENT
 
 
-def near_kernel(before, keep, newer, w_time, b_up, t0, t1, wc, wl, wr, done, t0_new, lhs, x, wide):
+def near_kernel(before, keep, newer, w_time, b_up, t1, wp, done, lhs, x, wide):
     rows = keep.shape[0] // 2
     cols = (newer.shape[0] - 2 * rows) // rows
     mine = lax.axis_index("tile")
@@ -186,17 +186,15 @@
     def _():
         t = t1[...] + dot(lhs[...], w_time[0])
         fill_x(t, mine, x, rows, cols)
-        convolve(x, wc, wl, wr, b_up, keep, mine, wide, done, rows, cols, [])
+        convolve(x, wp, b_up, keep, mine, wide, done, rows, cols, [])
 
     @pl.when(jnp.logical_not(valid))
     def _():
         done[...] = jnp.zeros_like(done)
 
-    t0_new[...] = t0[...] + dot(lhs[...], w_time[1])
-
 
 def far_kernel(
-    keep, near_before, far, w_time, b_up, t0, wc, wl, wr, second, out, lhs, x, wide, done, sems
+    keep, newer, near_before, far, w_time, b_up, t0, wp, second, out, lhs, x, wide, done, sems
 ):
     early = pltpu.make_async_copy(second, out.at[pl.ds(2, 2)], sems.at[LEAVES])
     early.start()
@@ -207,11 +205,13 @@
     two = is_there(near_before)
     older = jnp.where(two, near_before[...], far[...])
     none = (place_tm == 0) | ((place_tm == 1) & jnp.logical_not(two))
-    lhs[...] = jnp.where(none, jnp.zeros_like(older), older)
-    t = t0[...] + dot(lhs[...], w_time[0])
+    chans = older.shape[1]
+    lhs[:, pl.ds(0, chans)] = jnp.where(none, jnp.zeros_like(older), older)
+    lhs[:, pl.ds(chans, chans)] = jnp.where(place_tm == 0, jnp.zeros_like(older), newer[...])
+    t = t0[...] + dot(lhs[...], w_time[pl.ds(0, 2)].reshape(2 * chans, 2 * chans))
     fill_x(t, mine, x, rows, cols)
     copies = leave(done, out.at[pl.ds(0, 2)], sems)
-    convolve(x, wc, wl, wr, b_up, keep, mine, wide, done, rows, cols, copies)
+    convolve(x, wp, b_up, keep, mine, wide, done, rows, cols, copies)
     for copy in copies + [early]:
         copy.wait()
 
@@ -258,52 +258,50 @@
         name="pack",
     )(frame_counts, own, own_far)
     newer = lax.ppermute(latest, "tm", step(1))
-    far = lax.ppermute(latest, "tm", [(i, i + 2) for i in range(ring - 2)])
-    near_before = lax.ppermute(before, "tm", step(1))
+    far = lax.ppermute(latest, "tm", step(2))
+    near_before = lax.ppermute(before, "tm", [(i, i + 1) for i in range(ring - 1)])
     partial = shape((pixels + extra, 2 * chans), F32)
     scratch = [
-        pltpu.VMEM(frame.shape, BF16),
+        pltpu.VMEM((pixels + extra, 2 * chans), BF16),
         pltpu.VMEM(((cols + 2) * extra, 3 * chans), BF16),
         pltpu.VMEM((2, lanes // 128, extra, 128), F32),
         pltpu.VMEM((2, extra, lanes), BF16),
         pltpu.SemaphoreType.DMA((LEAVES + 1,)),
     ]
-    t0, t1, wc, wl, wr = pl.pallas_call(
+    t0, t1, wp = pl.pallas_call(
         local_kernel,
         out_shape=(
             partial,
             partial,
-            shape((2, 2 * outc, 2 * chans), BF16),
-            shape((2, 256, 2 * chans), BF16),
-            shape((2, 256, 2 * chans), BF16),
+            shape((2, 4 * outc, 2 * chans), BF16),
         ),
         in_specs=[VMEM] * 5,
-        out_specs=(VMEM,) * 5,
+        out_specs=(VMEM,) * 3,
         scratch_shapes=[pltpu.VMEM(frame.shape, BF16)],
         compiler_params=PARAMS,
         cost_estimate=cost(10**6, 1 << 10),
         name="local",
     )(latest, before, w_time, b_time, w_up)
-    second, t0 = pl.pallas_call(
+    second = pl.pallas_call(
         near_kernel,
-        out_shape=(shape((2, 2 * rows, lanes), BF16), partial),
-        in_specs=[VMEM] * 10,
-        out_specs=(VMEM, VMEM),
-        scratch_shapes=scratch[:3],
+        out_shape=shape((2, 2 * rows, lanes), BF16),
+        in_specs=[VMEM] * 7,
+        out_specs=VMEM,
+        scratch_shapes=[pltpu.VMEM(frame.shape, BF16)] + scratch[1:3],
         compiler_params=PARAMS,
         cost_estimate=cost(10**9, 4 << 20),
         name="near",
-    )(before, keep, newer, w_time, b_up, t0, t1, wc, wl, wr)
+    )(before, keep, newer, w_time, b_up, t1, wp)
     return pl.pallas_call(
         far_kernel,
         out_shape=shape((2 * slots, 2 * rows, lanes), BF16),
-        in_specs=[VMEM] * 10,
+        in_specs=[VMEM] * 9,
         out_specs=HBM,
         scratch_shapes=scratch,
         compiler_params=PARAMS,
         cost_estimate=cost(10**9, 4 << 20),
         name="far",
-    )(keep, near_before, far, w_time, b_up, t0, wc, wl, wr, second)
+    )(keep, newer, near_before, far, w_time, b_up, t0, wp, second)
 
 
 def solution(mesh):

time: 16.3 us -> 15.5 us (0.951)
  Pallas kernels: 6.44 us -> 6 us
  waiting for transfers between devices: 0.96 us -> 0.57 us
    pallas_call x2, Pallas kernels: 3.11 us -> 2.65 us  [the longest x1 1.33 us: per_device(): pl.pallas_call(local_kernel, out_shape=(partial, partial, shape((2, 4 * o...]
    ppermute x2, waiting for transfers between devices: 0.45 us -> 0.01 us  [the longest x1 0.01 us: per_device(): far = lax.ppermute(latest, 'tm', step(2))]
  transfers between devices with their start and end apart: 4 -> 4, of which waited for: 2 -> 1; matrix products, arithmetic and copies ran while one was open for 0% -> 0% of each run, Pallas kernels for 25% -> 24%
where the time goes in v5:
time: 15.5 us; the launch traced here: 15.4 us
  starting transfers between devices  8.02 us (52%)
  Pallas kernels  6 us (39%)
  between operations  0.75 us (5%)
  waiting for transfers between devices  0.57 us (4%)
    ppermute x1, starting transfers between devices, per_device(): lax.ppermute(before, 'tm', [(i, i + 1) for i in range(ring - 1)])  3.45 us
    ppermute x1, starting transfers between devices, per_device(): newer = lax.ppermute(latest, 'tm', step(1))  2.54 us
    pallas_call x1, Pallas kernels, per_device(): pl.pallas_call(far_kernel, out_shape=shape((2 * slots, 2 * rows, lanes),...  2.15 us
    ppermute x1, starting transfers between devices, per_device(): far = lax.ppermute(latest, 'tm', step(2))  1.58 us
    pallas_call x1, Pallas kernels, per_device(): pl.pallas_call(local_kernel, out_shape=(partial, partial, shape((2, 4 * o...  1.33 us
    pallas_call x1, Pallas kernels, per_device(): pl.pallas_call(near_kernel, out_shape=shape((2, 2 * rows, lanes), BF16),...  1.32 us
    pallas_call x1, Pallas kernels, per_device(): pl.pallas_call(load_kernel, out_shape=(shape((extra, 128), F32), shape(la...  0.99 us
    ppermute x1, waiting for transfers between devices, per_device(): newer = lax.ppermute(latest, 'tm', step(1))  0.56 us
  transfers between devices with their start and end apart: 4, of which 1 were waited for; matrix products, arithmetic and copies ran while one was open for 0% of the time, Pallas kernels for 24%

profile of v5, /device:TPU:0, one launch (start us, length us, event | category | flops | bytes accessed | tf_op | source)
XLA Modules:
  0.0 15.4 jit_solution(506371966277309740)
XLA Ops:
  0.0 0.5 %collective-permute-start = (bf16[2,8,16,384]{3,2,1,0:T(8,128)(2,1)}, bf16[2,8,16,384]{3,2,1,0:T(8,128)(2,1)S(1)}, u32[]{:S(2)}, u32[]{:S(2)}) collective-permute-start(bf16[2,8,16,384]{3,2,1,0:T(8,128)(2,1)} %own_hbm.1), channel_id=1, source_target_pairs={{0,1},{1,0},{2,3},{3,2},{4,5},{5,4},{6,7},{7,6},{8,9},{9,8},{10,11... | collective-permute-start | bytes 589832 | tf_op jit(solution)/shard_map/ppermute | solution.py:234
  1.1 1.0 %load.1 = (f32[16,128]{1,0:T(8,128)S(1)}, bf16[2,8,16,384]{3,2,1,0:T(8,128)(2,1)S(1)}, f32[768]{0:T(1024)S(1)}, f32[192]{0:T(256)S(1)}) custom-call(s32[16]{0:T(128)} %owners_hbm.1, bf16[2,8,16,384]{3,2,1,0:T(8,128)(2,1)} %own_hbm.1, f32[768]{0:T(1024)} %b_time_hbm.1, f32[192]{0:T(256)} %b_up_hbm.1), custom_call_target="tpu_custom_call" | custom-call | flops 1000000 | bytes 1024 | tf_op jit(solution)/shard_map/load/pallas_call | solution.py:235
  2.1 0.0 collective-permute-done.own_far
  2.1 0.0 copy-start
  2.1 0.0 copy-start.1
  2.1 0.2 %pack.1 = (bf16[144,384]{1,0:T(8,128)(2,1)S(1)}, bf16[144,384]{1,0:T(8,128)(2,1)S(1)}) custom-call(s32[1]{0:T(128)S(6)} %copy.8.counts, bf16[2,8,16,384]{3,2,1,0:T(8,128)(2,1)S(1)} %get-tuple-element.15.own, bf16[2,8,16,384]{3,2,1,0:T(8,128)(2,1)S(1)} %collective-permute-done.own_far), custom_call_target="tpu_custom_call" | custom-call | flops 3000000000 | bytes 1024 | tf_op jit(solution)/shard_map/pack/pallas_call | solution.py:251
  2.4 2.5 %collective-permute-start.1 = (bf16[144,384]{1,0:T(8,128)(2,1)S(1)}, bf16[144,384]{1,0:T(8,128)(2,1)S(1)}, u32[]{:S(2)}, u32[]{:S(2)}) collective-permute-start(bf16[144,384]{1,0:T(8,128)(2,1)S(1)} %get-tuple-element.16.latest), channel_id=1, source_target_pairs={{0,2},{2,4},{4,6},{6,8},{8,10},{10,12},{12,14},{14,0},{1,3},{3,5},... | collective-permute-start | bytes 331784 | tf_op jit(solution)/shard_map/ppermute | solution.py:260
  4.9 1.6 %collective-permute-start.3 = (bf16[144,384]{1,0:T(8,128)(2,1)S(1)}, bf16[144,384]{1,0:T(8,128)(2,1)S(1)}, u32[]{:S(2)}, u32[]{:S(2)}) collective-permute-start(bf16[144,384]{1,0:T(8,128)(2,1)S(1)} %get-tuple-element.16.latest), channel_id=1, source_target_pairs={{0,4},{2,6},{4,8},{6,10},{8,12},{10,14},{12,0},{14,2},{1,5},{3,7},... | collective-permute-start | bytes 331784 | tf_op jit(solution)/shard_map/ppermute | solution.py:261
  6.5 3.4 %collective-permute-start.2 = (bf16[144,384]{1,0:T(8,128)(2,1)S(1)}, bf16[144,384]{1,0:T(8,128)(2,1)S(1)}, u32[]{:S(2)}, u32[]{:S(2)}) collective-permute-start(bf16[144,384]{1,0:T(8,128)(2,1)S(1)} %get-tuple-element.17.before), channel_id=1, source_target_pairs={{0,2},{2,4},{4,6},{6,8},{8,10},{10,12},{12,14},{1,3},{3,5},{5,7},{... | collective-permute-start | bytes 331784 | tf_op jit(solution)/shard_map/ppermute | solution.py:262
  9.9 0.0 copy-done
  9.9 0.0 copy-done.1
  10.0 1.3 %local.1 = (f32[144,768]{1,0:T(8,128)S(1)}, f32[144,768]{1,0:T(8,128)S(1)}, bf16[2,768,768]{2,1,0:T(8,128)(2,1)S(1)}) custom-call(bf16[144,384]{1,0:T(8,128)(2,1)S(1)} %get-tuple-element.16.latest, bf16[144,384]{1,0:T(8,128)(2,1)S(1)} %get-tuple-element.17.before, bf16[3,384,768]{2,1,0:T(8,128)(2,1)S(1)} %copy-done, f32[768]{0:T(1024)S(1)} %get-tuple-element.19.b_time, ...), custom_call_target="tpu_custom_call" | custom-call | flops 1000000 | bytes 1024 | tf_op jit(solution)/shard_map/local/pallas_call | solution.py:271
  11.3 0.6 %collective-permute-done.1.newer = bf16[144,384]{1,0:T(8,128)(2,1)S(1)} collective-permute-done((bf16[144,384]{1,0:T(8,128)(2,1)S(1)}, bf16[144,384]{1,0:T(8,128)(2,1)S(1)}, u32[]{:S(2)}, u32[]{:S(2)}) %collective-permute-start.1) | collective-permute-done | bytes 110624 | tf_op jit(solution)/shard_map/ppermute | solution.py:260
  11.9 1.3 %near.1.second = bf16[2,16,6144]{2,1,0:T(8,128)(2,1)S(1)} custom-call(bf16[144,384]{1,0:T(8,128)(2,1)S(1)} %get-tuple-element.17.before, f32[16,128]{1,0:T(8,128)S(1)} %get-tuple-element.14.keep, bf16[144,384]{1,0:T(8,128)(2,1)S(1)} %collective-permute-done.1.newer, bf16[3,384,768]{2,1,0:T(8,128)(2,1)S(1)} %copy-done, f32[192]{0:T(256)S(1)} %get-tuple-element.18.b_up, ...), custom_call_target="tpu_custom_call" | custom-call | flops 1000000000 | bytes 4194304 | tf_op jit(solution)/shard_map/near/pallas_call | solution.py:285
  13.2 0.0 collective-permute-done.3.far
  13.2 0.0 collective-permute-done.2.near_before
  13.2 2.1 %far.1 = bf16[4,16,6144]{2,1,0:T(8,128)(2,1)} custom-call(f32[16,128]{1,0:T(8,128)S(1)} %get-tuple-element.14.keep, bf16[144,384]{1,0:T(8,128)(2,1)S(1)} %collective-permute-done.1.newer, bf16[144,384]{1,0:T(8,128)(2,1)S(1)} %collective-permute-done.2.near_before, bf16[144,384]{1,0:T(8,128)(2,1)S(1)} %collective-permute-done.3.far, ...), custom_call_target="tpu_custom_call" | custom-call | flops 1000000000 | bytes 4194304 | tf_op jit(solution)/shard_map/far/pallas_call | solution.py:295
Async XLA Ops:
  0.0 2.1 %collective-permute-start = (bf16[2,8,16,384]{3,2,1,0:T(8,128)(2,1)}, bf16[2,8,16,384]{3,2,1,0:T(8,128)(2,1)S(1)}, u32[]{:S(2)}, u32[]{:S(2)}) collective-permute-start(bf16[2,8,16,384]{3,2,1,0:T(8,128)(2,1)} %own_hbm.1), channel_id=1, source_target_pairs={{0,1},{1,0},{2,3},{3,2},{4,5},{5,4},{6,7},{7,6},{8,9},{9,8},{10,11... | collective-permute-start | bytes 589832 | tf_op jit(solution)/shard_map/ppermute | solution.py:234
  2.1 7.8 %copy-start = (bf16[3,384,768]{2,1,0:T(8,128)(2,1)S(1)}, bf16[3,384,768]{2,1,0:T(8,128)(2,1)}, u32[]{:S(2)}) copy-start(bf16[3,384,768]{2,1,0:T(8,128)(2,1)} %w_time.5) | copy-start | bytes 5308420
  2.1 7.8 %copy-start.1 = (bf16[3,3,384,192]{2,3,1,0:T(8,128)(2,1)S(1)}, bf16[3,3,384,192]{2,3,1,0:T(8,128)(2,1)}, u32[]{:S(2)}) copy-start(bf16[3,3,384,192]{2,3,1,0:T(8,128)(2,1)} %param.12) | copy-start | bytes 3981316
  2.4 9.5 %collective-permute-start.1 = (bf16[144,384]{1,0:T(8,128)(2,1)S(1)}, bf16[144,384]{1,0:T(8,128)(2,1)S(1)}, u32[]{:S(2)}, u32[]{:S(2)}) collective-permute-start(bf16[144,384]{1,0:T(8,128)(2,1)S(1)} %get-tuple-element.16.latest), channel_id=1, source_target_pairs={{0,2},{2,4},{4,6},{6,8},{8,10},{10,12},{12,14},{14,0},{1,3},{3,5},... | collective-permute-start | bytes 331784 | tf_op jit(solution)/shard_map/ppermute | solution.py:260
  4.9 8.3 %collective-permute-start.3 = (bf16[144,384]{1,0:T(8,128)(2,1)S(1)}, bf16[144,384]{1,0:T(8,128)(2,1)S(1)}, u32[]{:S(2)}, u32[]{:S(2)}) collective-permute-start(bf16[144,384]{1,0:T(8,128)(2,1)S(1)} %get-tuple-element.16.latest), channel_id=1, source_target_pairs={{0,4},{2,6},{4,8},{6,10},{8,12},{10,14},{12,0},{14,2},{1,5},{3,7},... | collective-permute-start | bytes 331784 | tf_op jit(solution)/shard_map/ppermute | solution.py:261
  6.5 6.7 %collective-permute-start.2 = (bf16[144,384]{1,0:T(8,128)(2,1)S(1)}, bf16[144,384]{1,0:T(8,128)(2,1)S(1)}, u32[]{:S(2)}, u32[]{:S(2)}) collective-permute-start(bf16[144,384]{1,0:T(8,128)(2,1)S(1)} %get-tuple-element.17.before), channel_id=1, source_target_pairs={{0,2},{2,4},{4,6},{6,8},{8,10},{10,12},{12,14},{1,3},{3,5},{5,7},{... | collective-permute-start | bytes 331784 | tf_op jit(solution)/shard_map/ppermute | solution.py:262
